TPU v7x, 512 devices: a whole 4x8x8 slice. The times are simulated.
512 devices in a mesh: plane: 32 (over x, z), tile: 16 (over y, core).
Axes of the slice: x: 4, y: 8, z: 8, core: 2. Of those that a mesh axis runs over, the one named last changes fastest.
Arguments:
- raw_planes: bfloat16 [3072, 512, 512], P('plane', 'tile'), may hold values from -6 to 6
- pair_sections: int32 [2048, 2], P('plane'), may hold values from 0 to 47
- pair_rows: int32 [2048, 2], P('plane'), may hold values from 0 to 128
- pair_extent: int32 [2048], P('plane'), may hold values from 64 to 128
- pair_owner: int32 [2048, 1], P('plane'), may hold values from 0 to 15; in each aligned block of 64 rows (0 to 63, 64 to 127, ...) at most 12 rows name the same one
Outputs:
- surface_out: bfloat16 [6144, 128, 256], P(('plane', 'tile'))
Inputs may be any that keep to these rules, and one draw needn't show every extreme that they name: `pair_owner`: among the 64 pairs of one slab no owner takes more than 12 pairs.
All inputs are finite; a program needn't handle non-finite values.
Results may differ from a plain program's by a relative error of at most 0.012.
The roundings to bfloat16 on the way count: a program that leaves them out, or rounds other values in their place, can miss the bound.
Values may be sent and summed in bfloat16 or wider, within the bound.
No kernel may reach another device: no remote copies, remote signals or barrier semaphores. Data moves between devices by JAX's collectives and lax.ppermute only.
A program may use at most 64 MiB of HBM per device.

v0:
```python
import math

import jax
import jax.numpy as jnp
import numpy as np
from jax import lax
from jax.experimental import pallas as pl
from jax.experimental.pallas import tpu as pltpu
from jax.sharding import PartitionSpec as P

BAND = 128
OWN_CAP = 12
FACE = 512
HALF = 256
TILES = 16
DEPTH = 8
FREQS = 8
GROUP = 8
VMEM_LIMIT = 24 * 1024 * 1024


def whole(space=pltpu.VMEM):
    return pl.BlockSpec(memory_space=space)


def params(**kw):
    return pltpu.CompilerParams(vmem_limit_bytes=VMEM_LIMIT, **kw)


def blur_weight(offset):
    offset = abs(offset)
    return (6.0, 4.0, 1.0)[offset] / 16.0 if offset <= 2 else 0.0


def blur_matrix():
    table = np.zeros((FACE, HALF), np.float32)
    for c in range(FACE):
        for j in range(HALF):
            if abs(c - 2 * j) <= 2:
                table[c, j] = blur_weight(c - 2 * j)
    return table.astype(jnp.bfloat16)


def dft_tables(length):
    indices = np.arange(length)
    phases = indices[:, None] * indices[None, :] % length
    angles = phases.astype(np.float32) * np.float32(2.0 * math.pi / length)
    factor = np.float32(1.0 / math.sqrt(length))
    return (
        (np.cos(angles) * factor).astype(jnp.bfloat16),
        (np.sin(angles) * factor).astype(jnp.bfloat16),
    )


def column_weights(first_tile):
    local = np.zeros((16, 32), np.float32)
    halo = np.zeros((16, 4), np.float32)
    for i in range(16):
        for c in range(32):
            local[i, c] = blur_weight(c + 2 - 2 * i)
        for h in range(4):
            halo[i, h] = blur_weight(h - 2 - 2 * i)
    if first_tile:
        local[0, 0] = 0.0
        halo[1, :] = 0.0
    return local, halo


def column_tables():
    grouped = np.zeros((2, GROUP * 16, GROUP * 36), np.float32)
    single = np.zeros((2, 16, 40), np.float32)
    for variant in (0, 1):
        local, halo = column_weights(variant == 0)
        for q in range(GROUP):
            rows = slice(q * 16, q * 16 + 16)
            grouped[variant, rows, q * 32 : q * 32 + 32] = local
            at = GROUP * 32 + q * 4
            grouped[variant, rows, at : at + 4] = halo
        single[variant, :, :32] = local
        single[variant, :, 36:40] = halo
    return grouped.astype(jnp.bfloat16), single.astype(jnp.bfloat16)


def row_transform_table():
    cos_half, sin_half = dft_tables(HALF)
    table = np.zeros((HALF, HALF), np.float32)
    for d in range(TILES):
        for f in range(FREQS):
            v = d * FREQS + f
            table[d * 16 + f] = cos_half[v]
            if v:
                table[d * 16 + FREQS + f] = -sin_half[v].astype(np.float32)
            else:
                table[d * 16 + FREQS + f] = cos_half[HALF // 2]
    return table.astype(jnp.bfloat16)


def row_inverse_table():
    cos_half, sin_half = dft_tables(HALF)
    table = np.zeros((HALF, HALF), np.float32)
    for v in range(HALF // 2):
        table[v] = cos_half[v].astype(np.float32) * (2.0 if v else 1.0)
        if v:
            table[HALF // 2 + v] = sin_half[v].astype(np.float32) * -2.0
        else:
            table[HALF // 2] = cos_half[HALF // 2]
    return table.astype(jnp.bfloat16)


def reversal():
    table = np.zeros((BAND, BAND), np.float32)
    for u in range(BAND):
        table[(BAND - u) % BAND, u] = 1.0
    return table.astype(jnp.bfloat16)


def dot(a, b):
    return jnp.dot(a, b, preferred_element_type=jnp.float32)


def dot_nt(a, b):
    return lax.dot_general(
        a, b, (((1,), (1,)), ((), ())), preferred_element_type=jnp.float32
    )


def across_kernel(raw_ref, table_hbm, across_ref, edge_ref, cells_ref, table_ref, sems):
    planes = raw_ref.shape[0]
    part = 16
    parts = planes // part
    ahead = 3

    def copy(k):
        held = pl.ds(k * part, part)
        return pltpu.make_async_copy(raw_ref.at[held], cells_ref.at[held], sems.at[k + 1])

    table_copy = pltpu.make_async_copy(table_hbm, table_ref, sems.at[0])
    table_copy.start()
    for k in range(ahead):
        copy(k).start()
    table_copy.wait()
    per = part // GROUP
    upper = lax.broadcasted_iota(jnp.int32, (8, HALF), 0) < 4
    for k in range(parts):
        copy(k).wait()
        if k + ahead < parts:
            copy(k + ahead).start()
        cells = cells_ref[k * part : (k + 1) * part].reshape(part * 32, FACE)
        across = dot(cells, table_ref[...])
        edges = []
        for q in range(0, part, 2):
            first = across[q * 32 + 24 : q * 32 + 32]
            second = across[q * 32 + 56 : q * 32 + 64]
            edges.append(jnp.where(upper, pltpu.roll(first, 4, 0), second))
        edges = jnp.concatenate(edges, axis=0).astype(jnp.bfloat16)
        edge_ref[k * per : (k + 1) * per] = edges.reshape(per, GROUP * 4, HALF)
        across = across.astype(jnp.bfloat16)
        across_ref[k * per : (k + 1) * per] = across.reshape(per, GROUP * 32, HALF)


def blur_across(raw, table):
    planes = raw.shape[0]
    groups = planes // GROUP
    return pl.pallas_call(
        across_kernel,
        in_specs=[whole(pltpu.HBM)] * 2,
        out_specs=[whole()] * 2,
        out_shape=[
            jax.ShapeDtypeStruct((groups, GROUP * 32, HALF), jnp.bfloat16),
            jax.ShapeDtypeStruct((groups, GROUP * 4, HALF), jnp.bfloat16),
        ],
        scratch_shapes=[
            pltpu.VMEM((planes, 32, FACE), jnp.bfloat16),
            pltpu.VMEM((FACE, HALF), jnp.bfloat16),
            pltpu.SemaphoreType.DMA((planes // 16 + 1,)),
        ],
        compiler_params=params(),
        cost_estimate=pl.CostEstimate(
            flops=2 * planes * 32 * FACE * HALF,
            bytes_accessed=planes * 32 * (FACE + HALF) * 2,
            transcendentals=0,
        ),
        name="blur_across",
    )(raw, table)


def last_kernel(tile_ref, across_ref, halo_ref, grouped_ref, out_ref):
    last = across_ref.shape[0] - 1
    stacked = jnp.concatenate([across_ref[last], halo_ref[last]], axis=0)
    weights = grouped_ref[jnp.minimum(tile_ref[0], 1), (GROUP - 1) * 16 :]
    out_ref[...] = dot(weights, stacked).astype(jnp.bfloat16)


def last_planar(tile, across, halo, grouped):
    return pl.pallas_call(
        last_kernel,
        in_specs=[whole(pltpu.SMEM)] + [whole()] * 3,
        out_specs=whole(),
        out_shape=jax.ShapeDtypeStruct((16, HALF), jnp.bfloat16),
        compiler_params=params(),
        name="last_planar",
    )(tile, across, halo, grouped)


def blend(before, middle, after):
    total = before.astype(jnp.float32) + 2.0 * middle.astype(jnp.float32)
    return ((total + after.astype(jnp.float32)) * 0.25).astype(jnp.bfloat16)


def section_kernel(
    tile_ref, across_ref, halo_ref, grouped_ref, table_ref, out_ref, head_ref, planar_ref
):
    groups = across_ref.shape[0]
    weights = grouped_ref[jnp.minimum(tile_ref[0], 1)]
    for g in range(groups):
        stacked = jnp.concatenate([across_ref[g], halo_ref[g]], axis=0)
        planar = dot(weights, stacked).astype(jnp.bfloat16)
        planar_ref[g * GROUP : (g + 1) * GROUP] = planar.reshape(GROUP, 16, HALF)
    head_ref[0] = planar_ref[0]
    head_ref[16] = planar_ref[1]
    table = table_ref[...]
    sections = groups * GROUP // 2
    for m in range(sections // 16):
        made = [
            blend(planar_ref[2 * s - 1], planar_ref[2 * s], planar_ref[2 * s + 1])
            for s in range(max(1, m * 16), (m + 1) * 16)
        ]
        if m == 0:
            for k in range(15):
                head_ref[1 + k] = made[k]
            continue
        rows = jnp.concatenate(made, axis=0)
        out_ref[:, m * HALF : (m + 1) * HALF] = dot_nt(table, rows).astype(jnp.bfloat16)


def row_spectra(tile, across, halo, grouped, table):
    planes = across.shape[0] * GROUP
    rows = planes // 2 * 16
    return pl.pallas_call(
        section_kernel,
        in_specs=[whole(pltpu.SMEM)] + [whole()] * 4,
        out_specs=[whole()] * 2,
        out_shape=[
            jax.ShapeDtypeStruct((HALF, rows), jnp.bfloat16),
            jax.ShapeDtypeStruct((17, 16, HALF), jnp.bfloat16),
        ],
        scratch_shapes=[pltpu.VMEM((planes, 16, HALF), jnp.bfloat16)],
        compiler_params=params(),
        cost_estimate=pl.CostEstimate(
            flops=2 * planes * 16 * 288 * HALF,
            bytes_accessed=planes * 32 * HALF * 2,
            transcendentals=0,
        ),
        name="row_spectra",
    )(tile, across, halo, grouped, table)


def head_kernel(
    tile_ref, slab_ref, next_ref, behind_ref, corner_ref, blur_ref, single_ref,
    head_ref, table_ref, spectra_ref, out_ref,
):
    rows = jnp.concatenate([behind_ref[...], corner_ref[24:]], axis=0)
    rows = dot(rows, blur_ref[...]).astype(jnp.bfloat16)
    weights = single_ref[jnp.minimum(tile_ref[0], 1)]
    far = dot(weights, rows)
    wrapped = lax.rem(slab_ref[0], DEPTH) == 0
    before = jnp.where(wrapped, far, next_ref[...].astype(jnp.float32))
    first = blend(before.astype(jnp.bfloat16), head_ref[0], head_ref[16])
    rows = jnp.concatenate([first] + [head_ref[k] for k in range(1, 16)], axis=0)
    out_ref[...] = dot_nt(table_ref[...], rows).astype(jnp.bfloat16)


def head_spectra(tile, slab, near, behind, corner, blur, single, head, table, spectra):
    return pl.pallas_call(
        head_kernel,
        grid=(1,),
        in_specs=[whole(pltpu.SMEM)] * 2 + [whole()] * 7 + [pl.BlockSpec(memory_space=pl.ANY)],
        out_specs=pl.BlockSpec((HALF, HALF), lambda g: (0, 0)),
        out_shape=jax.ShapeDtypeStruct(spectra.shape, jnp.bfloat16),
        input_output_aliases={9: 0},
        compiler_params=params(),
        name="head_spectra",
    )(tile, slab, near, behind, corner, blur, single, head, table, spectra)


def cross_kernel(
    tile_ref, meta_ref, spectra_ref, table_ref, out_ref, held_ref, band_ref
):
    pairs = meta_ref.shape[1]
    blocks = spectra_ref.shape[2] // 128
    lane = lax.broadcasted_iota(jnp.int32, (16, 128), 1)
    out_ref[...] = jnp.zeros_like(out_ref)
    for k in range(blocks):
        for h in range(2):
            a = [
                spectra_ref[8 * h + t, :, 128 * k : 128 * (k + 1)].astype(jnp.float32)
                for t in range(8)
            ]
            for bit in (1, 2, 4):
                low = (lane // 16) & bit == 0
                for i in range(8):
                    if i & bit:
                        continue
                    j = i + bit
                    first = jnp.where(low, a[i], pltpu.roll(a[j], 16 * bit, 1))
                    second = jnp.where(low, pltpu.roll(a[i], 128 - 16 * bit, 1), a[j])
                    a[i], a[j] = first, second
            for s in range(8):
                held_ref[8 * k + s, h] = a[s]

    batch = 8
    steps = pairs // batch
    eight = (FREQS, 128)
    column = lax.broadcasted_iota(jnp.int32, eight, 1)
    special = (lax.broadcasted_iota(jnp.int32, eight, 0) == 0) & (tile_ref[0] == 0)
    upper = column > BAND // 2

    def cut(step, buffer):
        for p in range(batch):
            n = step * batch + p
            live = lane < meta_ref[4, n]
            for side in range(2):
                which = meta_ref[side, n]
                start = meta_ref[2 + side, n]
                from_low = (lane >= start) | (lane < start - 128)
                mixed = jnp.where(from_low, held_ref[which, 0], held_ref[which, 1])
                turned = pltpu.roll(mixed, (256 - start) & 127, 1)
                band = jnp.where(live, turned, 0.0)
                band_ref[buffer, 2 * p + side] = band.astype(jnp.bfloat16)

    def cross(step, buffer):
        bands = band_ref[buffer].reshape(2 * batch * 16, 128)
        full = dot(bands, table_ref[...])
        for p in range(batch):
            real, imag, edge_real, edge_imag = [], [], [], []
            for side in range(2):
                at = (2 * p + side) * 16
                cos_re = full[at : at + 8, :128]
                sin_re = full[at : at + 8, 128:]
                cos_im = full[at + 8 : at + 16, :128]
                sin_im = full[at + 8 : at + 16, 128:]
                real.append(cos_re + jnp.where(special, 0.0, sin_im))
                imag.append(jnp.where(special, 0.0, cos_im) - sin_re)
                edge_real.append(cos_im)
                edge_imag.append(-sin_im)
            cross_real = real[0] * real[1] + imag[0] * imag[1]
            cross_imag = imag[0] * real[1] - real[0] * imag[1]
            last_real = edge_real[0] * edge_real[1] + edge_imag[0] * edge_imag[1]
            last_imag = edge_imag[0] * edge_real[1] - edge_real[0] * edge_imag[1]
            first_slot = jnp.where(special & upper, cross_imag, cross_real)
            packed = jnp.where(upper, last_imag, last_real)
            second_slot = jnp.where(special, packed, cross_imag)
            both = jnp.concatenate([first_slot, second_slot], axis=0)
            out_ref[meta_ref[5, step * batch + p]] = both.astype(jnp.bfloat16)

    cut(0, 0)

    def body(step, _):
        cross(step, step & 1)
        cut(step + 1, (step + 1) & 1)
        return 0

    lax.fori_loop(0, steps - 1, body, 0)
    cross(steps - 1, (steps - 1) & 1)


def pair_table(sections, rows, extents, owners):
    position = jnp.arange(owners.shape[0], dtype=jnp.int32)
    earlier = (owners[:, None] == owners[None, :]) & (position[None, :] < position[:, None])
    slots = jnp.sum(earlier.astype(jnp.int32), axis=1)
    places = owners * OWN_CAP + slots
    return jnp.concatenate([sections.T, rows.T + 1, extents[None], places[None]], axis=0)


def cross_spectra(tile, meta, spectra, table):
    held = spectra.shape[2] // 16
    return pl.pallas_call(
        cross_kernel,
        in_specs=[whole(pltpu.SMEM)] * 2 + [whole()] * 2,
        out_specs=whole(),
        out_shape=jax.ShapeDtypeStruct((TILES * OWN_CAP, 16, 128), jnp.bfloat16),
        scratch_shapes=[
            pltpu.VMEM((held, 2, 16, 128), jnp.float32),
            pltpu.VMEM((2, 16, 16, 128), jnp.bfloat16),
        ],
        compiler_params=params(),
        name="cross_spectra",
    )(tile, meta, spectra, table)


def surface_kernel(
    cross_ref, reversal_ref, column_ref, row_ref, out_hbm, turned_ref, size_ref,
    norm_ref, col_ref, out_ref, sems,
):
    lane = lax.broadcasted_iota(jnp.int32, (FREQS, 128), 1)
    top = lax.broadcasted_iota(jnp.int32, (FREQS, 128), 0) == 0
    edge = lax.broadcasted_iota(jnp.int32, (128, 128), 1) == 0
    upper = lane > BAND // 2
    ends = (lane == 0) | (lane == BAND // 2)

    turned = dot(cross_ref[0].reshape(OWN_CAP * 16, 128), reversal_ref[...])
    turned_ref[...] = turned.reshape(OWN_CAP, 16, 128)

    def unpack(packed, turned):
        real = jnp.where(upper, turned, packed)
        imag = jnp.where(upper, packed, jnp.where(ends, 0.0, -turned))
        return real, imag

    def rounded(value):
        return value.astype(jnp.bfloat16).astype(jnp.float32)

    def replaced(row, rows):
        return jnp.concatenate([jnp.where(top, row, rows[:8]), rows[8:]], axis=0)

    def parts(slot):
        block = cross_ref[:, slot].astype(jnp.float32)
        real = block[:, :8, :].reshape(128, 128)
        imag = block[:, 8:, :].reshape(128, 128)
        turned = turned_ref[slot]
        real_0, imag_0 = unpack(real[:8], turned[:8])
        real_n, imag_n = unpack(imag[:8], turned[8:])
        return replaced(real_0, real), replaced(imag_0, imag), real_n, imag_n

    def magnitude(real, imag):
        power = real * real + imag * imag
        return power * lax.rsqrt(jnp.maximum(power, 1e-30))

    means = []
    for slot in range(OWN_CAP):
        real, imag, real_n, imag_n = parts(slot)
        size = magnitude(real, imag)
        size_n = magnitude(real_n, imag_n)
        size_ref[slot, :128] = size
        size_ref[slot, 128:] = size_n
        total = 2.0 * jnp.sum(size.reshape(16, 8, 128), axis=0)
        total = jnp.sum(total + jnp.where(top, size_n - size[:8], 0.0))
        means.append(total / (BAND * HALF) + 1e-06)
    for slot in range(OWN_CAP):
        real, imag, real_n, imag_n = parts(slot)
        scale = 1.0 / (size_ref[slot, :128] + means[slot])
        scale_n = 1.0 / (size_ref[slot, 128:] + means[slot])
        norm_real = real * scale
        norm_imag = imag * scale
        zero = rounded(norm_real[:8]) - rounded(norm_imag[:8])
        last = rounded(real_n * scale_n) - rounded(imag_n * scale_n)
        norm_ref[slot, :128] = replaced(zero, norm_real).astype(jnp.bfloat16)
        norm_ref[slot, 128:] = replaced(last, norm_imag).astype(jnp.bfloat16)
    for slot in range(OWN_CAP):
        full = dot_nt(column_ref[...], norm_ref[slot])
        cos_re, cos_im = full[:128, :128], full[:128, 128:]
        sin_re, sin_im = full[128:, :128], full[128:, 128:]
        col_real = cos_re + jnp.where(edge, sin_re, -sin_im)
        col_imag = cos_im + jnp.where(edge, sin_im, sin_re)
        col_ref[slot, :, :128] = col_real.astype(jnp.bfloat16)
        col_ref[slot, :, 128:] = col_imag.astype(jnp.bfloat16)
    step = 3
    copies = []
    for k in range(OWN_CAP // step):
        held = slice(k * step, (k + 1) * step)
        made = dot(col_ref[held].reshape(step * BAND, HALF), row_ref[...])
        out_ref[held] = made.astype(jnp.bfloat16).reshape(step, BAND, HALF)
        held = pl.ds(k * step, step)
        copies.append(
            pltpu.make_async_copy(out_ref.at[held], out_hbm.at[held], sems.at[k])
        )
        copies[-1].start()
    for copy in copies:
        copy.wait()


def surfaces(cross, back, column, row):
    return pl.pallas_call(
        surface_kernel,
        in_specs=[whole()] * 4,
        out_specs=whole(pltpu.HBM),
        out_shape=jax.ShapeDtypeStruct((OWN_CAP, BAND, HALF), jnp.bfloat16),
        scratch_shapes=[
            pltpu.VMEM((OWN_CAP, 16, 128), jnp.float32),
            pltpu.VMEM((OWN_CAP, 136, 128), jnp.float32),
            pltpu.VMEM((OWN_CAP, HALF, 128), jnp.bfloat16),
            pltpu.VMEM((OWN_CAP, BAND, HALF), jnp.bfloat16),
            pltpu.VMEM((OWN_CAP, BAND, HALF), jnp.bfloat16),
            pltpu.SemaphoreType.DMA((4,)),
        ],
        compiler_params=params(),
        name="surfaces",
    )(cross, back, column, row)


def correlate(raw_planes, pair_sections, pair_rows, pair_extent, pair_owner):
    tile = lax.axis_index("tile").astype(jnp.int32).reshape(1)
    slab = lax.axis_index("plane").astype(jnp.int32).reshape(1)
    slabs = lax.axis_size("plane")
    planes = raw_planes.shape[0]
    owners = pair_owner[:, 0]

    far = [s for s in range(slabs - 1) if (s + 1) % DEPTH == 0]
    near = [s for s in range(slabs - 1) if (s + 1) % DEPTH]
    turns = [(t, (t + 1) % TILES) for t in range(TILES)]
    corners = [(s * TILES + t, (s + 1) * TILES + u) for s in far for t, u in turns]
    last = raw_planes[planes - 1]
    behind = lax.ppermute(last, "plane", [(s, s + 1) for s in far])
    corner = lax.ppermute(last, ("plane", "tile"), corners)
    table = pltpu.with_memory_space_constraint(jnp.asarray(blur_matrix()), pltpu.HBM)
    held = pltpu.with_memory_space_constraint(raw_planes, pltpu.HBM)
    across, edges = blur_across(held, table)
    halo = lax.ppermute(edges, "tile", turns)
    grouped, single = column_tables()
    meta = pair_table(pair_sections, pair_rows, pair_extent, owners)
    last = last_planar(tile, across, halo, grouped)
    last = lax.ppermute(last, "plane", [(s, s + 1) for s in near])
    spectra, head = row_spectra(tile, across, halo, grouped, row_transform_table())
    spectra = head_spectra(
        tile, slab, last, behind, corner, blur_matrix(), single, head,
        row_transform_table(), spectra,
    )
    spectra, meta = lax.optimization_barrier((spectra, meta))
    spectra = lax.all_to_all(
        spectra.reshape(TILES, 16, spectra.shape[1]), "tile", 0, 0, tiled=True
    )

    cos_band, sin_band = dft_tables(BAND)
    cross = cross_spectra(
        tile, meta, spectra, np.concatenate([cos_band, sin_band], axis=1)
    )
    cross = lax.all_to_all(
        cross.reshape(TILES, OWN_CAP * 16, 128), "tile", 0, 0, tiled=True
    )
    return surfaces(
        cross.reshape(TILES, OWN_CAP, 16, 128),
        reversal(),
        np.concatenate([cos_band, sin_band], axis=0),
        row_inverse_table(),
    )


def solution(mesh):
    return jax.shard_map(
        correlate,
        mesh=mesh,
        in_specs=(
            P("plane", "tile", None),
            P("plane", None),
            P("plane", None),
            P("plane"),
            P("plane", None),
        ),
        out_specs=P(("plane", "tile"), None, None),
        check_vma=False,
    )
```

profile of v0, /device:TPU:7, one launch (start us, length us, event | category | flops | bytes accessed | tf_op | source)
XLA Modules:
  0.0 71.9 jit_solution(15949789193710505526)
XLA Ops:
  0.0 0.0 copy-start.11
  0.0 0.0 copy-start.8
  0.0 0.0 copy-start.10
  0.0 0.9 %slice_bitcast_fusion = bf16[32,512]{1,0:T(8,128)(2,1)S(1)} fusion(bf16[96,32,512]{2,1,0:T(8,128)(2,1)} %raw_ref.1), kind=kLoop, calls=%fused_computation.2 | loop fusion | bytes 65536 | tf_op jit(solution)/shard_map/squeeze | solution.py:501
  0.9 1.4 %collective-permute-start.2 = (bf16[32,512]{1,0:T(8,128)(2,1)S(1)}, bf16[32,512]{1,0:T(8,128)(2,1)S(1)}, u32[]{:S(2)}, u32[]{:S(2)}) collective-permute-start(bf16[32,512]{1,0:T(8,128)(2,1)S(1)} %slice_bitcast_fusion), channel_id=1, source_target_pairs={{112,128},{240,256},{368,384},{113,129},{241,257},{369,385},{114,1... | collective-permute-start | bytes 98312 | tf_op jit(solution)/shard_map/ppermute | solution.py:502
  2.3 1.3 %collective-permute-start.3 = (bf16[32,512]{1,0:T(8,128)(2,1)S(1)}, bf16[32,512]{1,0:T(8,128)(2,1)S(1)}, u32[]{:S(2)}, u32[]{:S(2)}) collective-permute-start(bf16[32,512]{1,0:T(8,128)(2,1)S(1)} %slice_bitcast_fusion), channel_id=1, source_target_pairs={{112,129},{113,130},{114,131},{115,132},{116,133},{117,134},{118,1... | collective-permute-start | bytes 98312 | tf_op jit(solution)/shard_map/ppermute | solution.py:503
  3.6 3.7 %blur_across.1 = (bf16[12,256,256]{2,1,0:T(8,128)(2,1)S(1)}, bf16[12,32,256]{2,1,0:T(8,128)(2,1)S(1)}) custom-call(bf16[96,32,512]{2,1,0:T(8,128)(2,1)} %raw_ref.1, bf16[512,256]{1,0:T(8,128)(2,1)} %constant.31.clone.table_hbm.blur_ref), custom_call_target="tpu_custom_call" | custom-call | flops 805306368 | bytes 4718592 | tf_op jit(solution)/shard_map/blur_across/pallas_call | solution.py:164
  7.4 1.9 %collective-permute-start = (bf16[12,32,256]{2,1,0:T(8,128)(2,1)S(1)}, bf16[12,32,256]{2,1,0:T(8,128)(2,1)S(1)}, u32[]{:S(2)}, u32[]{:S(2)}) collective-permute-start(bf16[12,32,256]{2,1,0:T(8,128)(2,1)S(1)} %get-tuple-element.12), channel_id=1, source_target_pairs={{0,1},{1,2},{2,3},{3,4},{4,5},{5,6},{6,7},{7,8},{8,9},{9,10},{10,1... | collective-permute-start | bytes 589832 | tf_op jit(solution)/shard_map/ppermute | solution.py:507
  9.2 0.0 copy-done.9
  9.3 0.0 copy-done.11
  9.3 0.2 convert_reduce_fusion
  9.4 0.0 copy-done.8
  9.5 0.0 copy-done.10
  9.5 0.0 copy-start.5
  9.5 2.4 %collective-permute-done.halo_ref = bf16[12,32,256]{2,1,0:T(8,128)(2,1)S(1)} collective-permute-done((bf16[12,32,256]{2,1,0:T(8,128)(2,1)S(1)}, bf16[12,32,256]{2,1,0:T(8,128)(2,1)S(1)}, u32[]{:S(2)}, u32[]{:S(2)}) %collective-permute-start) | collective-permute-done | bytes 196640 | tf_op jit(solution)/shard_map/ppermute | solution.py:507
  11.9 0.0 copy-done.1
  11.9 0.1 last_planar.1
  12.0 0.0 copy-start.4
  12.0 0.0 copy-start.6
  12.0 2.9 %collective-permute-start.1 = (bf16[16,256]{1,0:T(8,128)(2,1)S(1)}, bf16[16,256]{1,0:T(8,128)(2,1)S(1)}, u32[]{:S(2)}, u32[]{:S(2)}) collective-permute-start(bf16[16,256]{1,0:T(8,128)(2,1)S(1)} %last_planar.1), channel_id=1, source_target_pairs={{0,16},{16,32},{32,48},{48,64},{64,80},{80,96},{96,112},{128,144},... | collective-permute-start | bytes 24584 | tf_op jit(solution)/shard_map/ppermute | solution.py:511
  14.9 0.0 copy-done.2
  14.9 0.8 %row_spectra.1 = (bf16[256,768]{1,0:T(8,128)(2,1)S(1)}, bf16[17,16,256]{2,1,0:T(8,128)(2,1)S(1)}) custom-call(s32[1]{0:T(128)} %bitcast.tile_ref, bf16[12,256,256]{2,1,0:T(8,128)(2,1)S(1)} %get-tuple-element.11.across_ref, bf16[12,32,256]{2,1,0:T(8,128)(2,1)S(1)} %collective-permute-done.halo_ref, bf16[2,128,288]{2,1,0:T(8,128)(2,1)S(1)} %copy-done.1, ...), custom_call_target="tpu_custom_call" | custom-call | flops 226492416 | bytes 1572864 | tf_op jit(solution)/shard_map/row_spectra/pallas_call | solution.py:239
  15.7 0.0 collective-permute-done.2.behind_ref
  15.7 0.0 collective-permute-done.3.corner_ref
  15.7 0.0 collective-permute-done.1.next_ref
  15.7 0.0 copy-done
  15.8 0.6 head_spectra.1
  16.3 24.7 %all_to_all.10.spectra_ref = bf16[16,16,768]{2,1,0:T(8,128)(2,1)S(1)} all-to-all(bf16[16,16,768]{2,1,0:T(8,128)(2,1)S(1)} %bitcast.18), channel_id=1, replica_groups=mesh['plane'=32,'tile'=16] {'tile'}, dimensions={0} | all-to-all | bytes 786432 | tf_op jit(solution)/shard_map/all_to_all | solution.py:518
  41.0 0.0 copy-done.5
  41.0 3.4 %cross_spectra.1 = bf16[192,16,128]{2,1,0:T(8,128)(2,1)S(1)} custom-call(s32[1]{0:T(128)} %bitcast.tile_ref, s32[6,64]{1,0:T(8,128)S(1)} %pad_add_fusion.meta_ref, bf16[16,16,768]{2,1,0:T(8,128)(2,1)S(1)} %all_to_all.10.spectra_ref, bf16[128,256]{1,0:T(8,128)(2,1)S(1)} %copy-done.5), custom_call_target="tpu_custom_call" | custom-call | tf_op jit(solution)/shard_map/cross_spectra/pallas_call | solution.py:377
  44.4 25.5 %all_to_all.11 = bf16[16,192,128]{2,1,0:T(8,128)(2,1)S(1)} all-to-all(bf16[16,192,128]{2,1,0:T(8,128)(2,1)S(1)} %bitcast.17), channel_id=1, replica_groups=mesh['plane'=32,'tile'=16] {'tile'}, dimensions={0} | all-to-all | bytes 1572864 | tf_op jit(solution)/shard_map/all_to_all | solution.py:526
  70.0 2.0 %surfaces.1 = bf16[12,128,256]{2,1,0:T(8,128)(2,1)} custom-call(bf16[16,12,16,128]{3,2,1,0:T(8,128)(2,1)S(1)} %bitcast.16, bf16[128,128]{1,0:T(8,128)(2,1)S(1)} %copy-done.6, bf16[256,128]{1,0:T(8,128)(2,1)S(1)} %copy-done.4, bf16[256,256]{1,0:T(8,128)(2,1)S(1)} %copy-done.3), custom_call_target="tpu_custom_call" | custom-call | tf_op jit(solution)/shard_map/surfaces/pallas_call | solution.py:472
  (13 shorter events, 0.0 us)
Async XLA Ops:
  0.0 11.9 %copy-start.1 = (bf16[2,128,288]{2,1,0:T(8,128)(2,1)S(1)}, bf16[2,128,288]{2,1,0:T(8,128)(2,1)}, u32[]{:S(2)}) copy-start(bf16[2,128,288]{2,1,0:T(8,128)(2,1)} %constant.32.clone.grouped_ref) | copy-start | bytes 442372
  0.0 14.9 %copy-start.2 = (bf16[256,256]{1,0:T(8,128)(2,1)S(1)}, bf16[256,256]{1,0:T(8,128)(2,1)}, u32[]{:S(2)}) copy-start(bf16[256,256]{1,0:T(8,128)(2,1)} %constant.33.clone.table_ref) | copy-start | bytes 393220
  0.0 9.2 %copy-start.9 = (s32[64,2]{0,1:T(2,128)S(1)}, s32[64,2]{0,1:T(2,128)}, u32[]{:S(2)}) copy-start(s32[64,2]{0,1:T(2,128)} %param.17) | copy-start | bytes 1540
  0.0 9.2 %copy-start.11 = (s32[64,1]{0,1:T(1,128)S(1)}, s32[64,1]{0,1:T(1,128)}, u32[]{:S(2)}) copy-start(s32[64,1]{0,1:T(1,128)} %param.19) | copy-start | bytes 772
  0.0 9.4 %copy-start.8 = (s32[64,2]{0,1:T(2,128)S(1)}, s32[64,2]{0,1:T(2,128)}, u32[]{:S(2)}) copy-start(s32[64,2]{0,1:T(2,128)} %param.16) | copy-start | bytes 1540
  0.0 9.4 %copy-start.10 = (s32[64]{0:T(128)S(1)}, s32[64]{0:T(128)}, u32[]{:S(2)}) copy-start(s32[64]{0:T(128)} %param.18) | copy-start | bytes 772
  0.9 14.8 %copy-start = (bf16[512,256]{1,0:T(8,128)(2,1)S(1)}, bf16[512,256]{1,0:T(8,128)(2,1)}, u32[]{:S(2)}) copy-start(bf16[512,256]{1,0:T(8,128)(2,1)} %constant.31.clone.table_hbm.blur_ref) | copy-start | bytes 786436
  0.9 14.8 %copy-start.7 = (bf16[2,16,40]{2,1,0:T(8,128)(2,1)S(1)}, bf16[2,16,40]{2,1,0:T(8,128)(2,1)}, u32[]{:S(2)}) copy-start(bf16[2,16,40]{2,1,0:T(8,128)(2,1)} %constant.34.clone.single_ref) | copy-start | bytes 7684
  0.9 14.8 %collective-permute-start.2 = (bf16[32,512]{1,0:T(8,128)(2,1)S(1)}, bf16[32,512]{1,0:T(8,128)(2,1)S(1)}, u32[]{:S(2)}, u32[]{:S(2)}) collective-permute-start(bf16[32,512]{1,0:T(8,128)(2,1)S(1)} %slice_bitcast_fusion), channel_id=1, source_target_pairs={{112,128},{240,256},{368,384},{113,129},{241,257},{369,385},{114,1... | collective-permute-start | bytes 98312 | tf_op jit(solution)/shard_map/ppermute | solution.py:502
  2.3 13.4 %collective-permute-start.3 = (bf16[32,512]{1,0:T(8,128)(2,1)S(1)}, bf16[32,512]{1,0:T(8,128)(2,1)S(1)}, u32[]{:S(2)}, u32[]{:S(2)}) collective-permute-start(bf16[32,512]{1,0:T(8,128)(2,1)S(1)} %slice_bitcast_fusion), channel_id=1, source_target_pairs={{112,129},{113,130},{114,131},{115,132},{116,133},{117,134},{118,1... | collective-permute-start | bytes 98312 | tf_op jit(solution)/shard_map/ppermute | solution.py:503
  7.4 4.5 %collective-permute-start = (bf16[12,32,256]{2,1,0:T(8,128)(2,1)S(1)}, bf16[12,32,256]{2,1,0:T(8,128)(2,1)S(1)}, u32[]{:S(2)}, u32[]{:S(2)}) collective-permute-start(bf16[12,32,256]{2,1,0:T(8,128)(2,1)S(1)} %get-tuple-element.12), channel_id=1, source_target_pairs={{0,1},{1,2},{2,3},{3,4},{4,5},{5,6},{6,7},{7,8},{8,9},{9,10},{10,1... | collective-permute-start | bytes 589832 | tf_op jit(solution)/shard_map/ppermute | solution.py:507
  9.5 31.6 %copy-start.5 = (bf16[128,256]{1,0:T(8,128)(2,1)S(1)}, bf16[128,256]{1,0:T(8,128)(2,1)}, u32[]{:S(2)}) copy-start(bf16[128,256]{1,0:T(8,128)(2,1)} %constant.35.clone.table_ref) | copy-start | bytes 196612
  12.0 58.0 %copy-start.3 = (bf16[256,256]{1,0:T(8,128)(2,1)S(1)}, bf16[256,256]{1,0:T(8,128)(2,1)}, u32[]{:S(2)}) copy-start(bf16[256,256]{1,0:T(8,128)(2,1)} %constant.38.clone.row_ref) | copy-start | bytes 393220
  12.0 58.0 %copy-start.4 = (bf16[256,128]{1,0:T(8,128)(2,1)S(1)}, bf16[256,128]{1,0:T(8,128)(2,1)}, u32[]{:S(2)}) copy-start(bf16[256,128]{1,0:T(8,128)(2,1)} %constant.37.clone.column_ref) | copy-start | bytes 196612
  12.0 57.9 %copy-start.6 = (bf16[128,128]{1,0:T(8,128)(2,1)S(1)}, bf16[128,128]{1,0:T(8,128)(2,1)}, u32[]{:S(2)}) copy-start(bf16[128,128]{1,0:T(8,128)(2,1)} %constant.36.clone.reversal_ref) | copy-start | bytes 98308
  12.0 3.7 %collective-permute-start.1 = (bf16[16,256]{1,0:T(8,128)(2,1)S(1)}, bf16[16,256]{1,0:T(8,128)(2,1)S(1)}, u32[]{:S(2)}, u32[]{:S(2)}) collective-permute-start(bf16[16,256]{1,0:T(8,128)(2,1)S(1)} %last_planar.1), channel_id=1, source_target_pairs={{0,16},{16,32},{32,48},{48,64},{64,80},{80,96},{96,112},{128,144},... | collective-permute-start | bytes 24584 | tf_op jit(solution)/shard_map/ppermute | solution.py:511
where the time goes:
time: 73.4 us; the launch traced here: 71.9 us
  blocking collectives  50.2 us (68%)
  Pallas kernels  10.6 us (14%)
  starting transfers between devices  7.44 us (10%)
  waiting for transfers between devices  2.37 us (3%)
  local copies, waits for them, and re-layouts  0.96 us (1%)
    all_to_all x1, blocking collectives, correlate(): lax.all_to_all(cross.reshape(TILES, OWN_CAP * 16, 128), 'tile', 0, 0, til...  25.5 us
    all_to_all x1, blocking collectives, correlate(): lax.all_to_all(spectra.reshape(TILES, 16, spectra.shape[1]), 'tile', 0, 0...  24.7 us
    pallas_call x1, Pallas kernels, blur_across(): pl.pallas_call(across_kernel, in_specs=[whole(pltpu.HBM)] * 2, out_specs=...  3.72 us
    pallas_call x1, Pallas kernels, cross_spectra(): pl.pallas_call(cross_kernel, in_specs=[whole(pltpu.SMEM)] * 2 + [whole()]...  3.41 us
    ppermute x1, starting transfers between devices, correlate(): last = lax.ppermute(last, 'plane', [(s, s + 1) for s in near])  2.87 us
    ppermute x1, waiting for transfers between devices, correlate(): halo = lax.ppermute(edges, 'tile', turns)  2.36 us
    pallas_call x1, Pallas kernels, surfaces(): pl.pallas_call(surface_kernel, in_specs=[whole()] * 4, out_specs=whole(pl...  2 us
    ppermute x1, starting transfers between devices, correlate(): halo = lax.ppermute(edges, 'tile', turns)  1.87 us
  transfers between devices with their start and end apart: 4, of which 1 were waited for; matrix products, arithmetic and copies ran while one was open for 0% of the time, Pallas kernels for 6%

commit v1 on v0

--- a/solution.py
+++ b/solution.py
@@ -124,56 +124,81 @@
     )
 
 
-def across_kernel(raw_ref, table_hbm, across_ref, edge_ref, cells_ref, table_ref, sems):
+def edge_kernel(raw_ref, table_hbm, edge_ref, last_ref, strip_ref, table_ref, sems):
     planes = raw_ref.shape[0]
-    part = 16
-    parts = planes // part
-    ahead = 3
-
-    def copy(k):
+    part = 32
+    copies = []
+    for k in range(planes // part):
         held = pl.ds(k * part, part)
-        return pltpu.make_async_copy(raw_ref.at[held], cells_ref.at[held], sems.at[k + 1])
-
-    table_copy = pltpu.make_async_copy(table_hbm, table_ref, sems.at[0])
-    table_copy.start()
-    for k in range(ahead):
-        copy(k).start()
-    table_copy.wait()
+        copies.append(
+            pltpu.make_async_copy(
+                raw_ref.at[held, pl.ds(24, 8), :], strip_ref.at[held], sems.at[k]
+            )
+        )
+    copies.insert(1, pltpu.make_async_copy(table_hbm, table_ref, sems.at[planes // part]))
+    copies.append(
+        pltpu.make_async_copy(raw_ref.at[planes - 1], last_ref, sems.at[planes // part + 1])
+    )
+    for copy in copies:
+        copy.start()
+    upper = lax.broadcasted_iota(jnp.int32, (8, HALF), 0) < 4
     per = part // GROUP
-    upper = lax.broadcasted_iota(jnp.int32, (8, HALF), 0) < 4
-    for k in range(parts):
-        copy(k).wait()
-        if k + ahead < parts:
-            copy(k + ahead).start()
-        cells = cells_ref[k * part : (k + 1) * part].reshape(part * 32, FACE)
+    copies.pop(1).wait()
+    for k in range(planes // part):
+        copies[k].wait()
+        cells = strip_ref[k * part : (k + 1) * part].reshape(part * 8, FACE)
         across = dot(cells, table_ref[...])
         edges = []
-        for q in range(0, part, 2):
-            first = across[q * 32 + 24 : q * 32 + 32]
-            second = across[q * 32 + 56 : q * 32 + 64]
-            edges.append(jnp.where(upper, pltpu.roll(first, 4, 0), second))
+        for q in range(0, part * 8, 16):
+            turned = pltpu.roll(across[q : q + 8], 4, 0)
+            edges.append(jnp.where(upper, turned, across[q + 8 : q + 16]))
         edges = jnp.concatenate(edges, axis=0).astype(jnp.bfloat16)
         edge_ref[k * per : (k + 1) * per] = edges.reshape(per, GROUP * 4, HALF)
-        across = across.astype(jnp.bfloat16)
-        across_ref[k * per : (k + 1) * per] = across.reshape(per, GROUP * 32, HALF)
-
-
-def blur_across(raw, table):
+    copies[-1].wait()
+
+
+def blur_edges(raw, table):
     planes = raw.shape[0]
-    groups = planes // GROUP
-    return pl.pallas_call(
-        across_kernel,
+    return pl.pallas_call(
+        edge_kernel,
         in_specs=[whole(pltpu.HBM)] * 2,
         out_specs=[whole()] * 2,
         out_shape=[
-            jax.ShapeDtypeStruct((groups, GROUP * 32, HALF), jnp.bfloat16),
-            jax.ShapeDtypeStruct((groups, GROUP * 4, HALF), jnp.bfloat16),
+            jax.ShapeDtypeStruct((planes // GROUP, GROUP * 4, HALF), jnp.bfloat16),
+            jax.ShapeDtypeStruct((32, FACE), jnp.bfloat16),
         ],
         scratch_shapes=[
-            pltpu.VMEM((planes, 32, FACE), jnp.bfloat16),
+            pltpu.VMEM((planes, 8, FACE), jnp.bfloat16),
             pltpu.VMEM((FACE, HALF), jnp.bfloat16),
-            pltpu.SemaphoreType.DMA((planes // 16 + 1,)),
+            pltpu.SemaphoreType.DMA((planes // 32 + 2,)),
         ],
+        compiler_params=params(),
+        cost_estimate=pl.CostEstimate(
+            flops=2 * planes * 8 * FACE * HALF,
+            bytes_accessed=planes * 8 * FACE * 2,
+            transcendentals=0,
+        ),
+        name="blur_edges",
+    )(raw, table)
+
+
+def across_kernel(raw_ref, table_ref, across_ref):
+    planes = raw_ref.shape[0]
+    part = 16
+    per = part // GROUP
+    for k in range(planes // part):
+        cells = raw_ref[k * part : (k + 1) * part].reshape(part * 32, FACE)
+        across = dot(cells, table_ref[...]).astype(jnp.bfloat16)
+        across_ref[k * per : (k + 1) * per] = across.reshape(per, GROUP * 32, HALF)
+
+
+def blur_across(raw, table):
+    planes = raw.shape[0]
+    return pl.pallas_call(
+        across_kernel,
+        in_specs=[whole()] * 2,
+        out_specs=whole(),
+        out_shape=jax.ShapeDtypeStruct((planes // GROUP, GROUP * 32, HALF), jnp.bfloat16),
         compiler_params=params(),
         cost_estimate=pl.CostEstimate(
             flops=2 * planes * 32 * FACE * HALF,
@@ -308,7 +333,7 @@
             for s in range(8):
                 held_ref[8 * k + s, h] = a[s]
 
-    batch = 8
+    batch = 32
     steps = pairs // batch
     eight = (FREQS, 128)
     column = lax.broadcasted_iota(jnp.int32, eight, 1)
@@ -381,7 +406,7 @@
         out_shape=jax.ShapeDtypeStruct((TILES * OWN_CAP, 16, 128), jnp.bfloat16),
         scratch_shapes=[
             pltpu.VMEM((held, 2, 16, 128), jnp.float32),
-            pltpu.VMEM((2, 16, 16, 128), jnp.bfloat16),
+            pltpu.VMEM((2, 64, 16, 128), jnp.bfloat16),
         ],
         compiler_params=params(),
         name="cross_spectra",
@@ -491,20 +516,19 @@
     tile = lax.axis_index("tile").astype(jnp.int32).reshape(1)
     slab = lax.axis_index("plane").astype(jnp.int32).reshape(1)
     slabs = lax.axis_size("plane")
-    planes = raw_planes.shape[0]
     owners = pair_owner[:, 0]
 
     far = [s for s in range(slabs - 1) if (s + 1) % DEPTH == 0]
     near = [s for s in range(slabs - 1) if (s + 1) % DEPTH]
     turns = [(t, (t + 1) % TILES) for t in range(TILES)]
     corners = [(s * TILES + t, (s + 1) * TILES + u) for s in far for t, u in turns]
-    last = raw_planes[planes - 1]
+    table = pltpu.with_memory_space_constraint(jnp.asarray(blur_matrix()), pltpu.HBM)
+    held = pltpu.with_memory_space_constraint(raw_planes, pltpu.HBM)
+    edges, last = blur_edges(held, table)
+    halo = lax.ppermute(edges, "tile", turns)
     behind = lax.ppermute(last, "plane", [(s, s + 1) for s in far])
     corner = lax.ppermute(last, ("plane", "tile"), corners)
-    table = pltpu.with_memory_space_constraint(jnp.asarray(blur_matrix()), pltpu.HBM)
-    held = pltpu.with_memory_space_constraint(raw_planes, pltpu.HBM)
-    across, edges = blur_across(held, table)
-    halo = lax.ppermute(edges, "tile", turns)
+    across = blur_across(raw_planes, blur_matrix())
     grouped, single = column_tables()
     meta = pair_table(pair_sections, pair_rows, pair_extent, owners)
     last = last_planar(tile, across, halo, grouped)

time: 73.4 us -> 69.4 us (0.946)
  the two profiles are of different devices: /device:TPU:7 before, /device:TPU:199 now
where the time goes in v1:
time: 69.4 us; the launch traced here: 69.2 us
  blocking collectives  50.2 us (72%)
  starting transfers between devices  8.67 us (12%)
  Pallas kernels  8.45 us (12%)
  waiting for transfers between devices  1.34 us (2%)
    all_to_all x1, blocking collectives, correlate(): lax.all_to_all(cross.reshape(TILES, OWN_CAP * 16, 128), 'tile', 0, 0, til...  25.5 us
    all_to_all x1, blocking collectives, correlate(): lax.all_to_all(spectra.reshape(TILES, 16, spectra.shape[1]), 'tile', 0, 0...  24.7 us
    ppermute x1, starting transfers between devices, correlate(): last = lax.ppermute(last, 'plane', [(s, s + 1) for s in near])  5.34 us
    pallas_call x1, Pallas kernels, blur_edges(): pl.pallas_call(edge_kernel, in_specs=[whole(pltpu.HBM)] * 2, out_specs=[w...  2.03 us
    pallas_call x1, Pallas kernels, surfaces(): pl.pallas_call(surface_kernel, in_specs=[whole()] * 4, out_specs=whole(pl...  2 us
    pallas_call x1, Pallas kernels, cross_spectra(): pl.pallas_call(cross_kernel, in_specs=[whole(pltpu.SMEM)] * 2 + [whole()]...  1.99 us
    ppermute x1, starting transfers between devices, correlate(): halo = lax.ppermute(edges, 'tile', turns)  1.87 us
  transfers between devices with their start and end apart: 4, of which 1 were waited for; matrix products, arithmetic and copies ran while one was open for 0% of the time, Pallas kernels for 3%

profile of v1, /device:TPU:199, one launch (start us, length us, event | category | flops | bytes accessed | tf_op | source)
XLA Modules:
  0.0 69.2 jit_solution(14698599779623721030)
XLA Ops:
  0.0 0.0 copy-start.12
  0.0 0.0 copy-start.9
  0.0 2.0 %blur_edges.1 = (bf16[12,32,256]{2,1,0:T(8,128)(2,1)S(1)}, bf16[32,512]{1,0:T(8,128)(2,1)S(1)}) custom-call(bf16[96,32,512]{2,1,0:T(8,128)(2,1)} %raw_ref.3, bf16[512,256]{1,0:T(8,128)(2,1)} %constant.31.clone.table_ref.table_hbm.blur_ref), custom_call_target="tpu_custom_call" | custom-call | flops 201326592 | bytes 786432 | tf_op jit(solution)/shard_map/blur_edges/pallas_call | solution.py:162
  2.1 0.0 copy-start.2
  2.1 0.8 %collective-permute-start.2 = (bf16[32,512]{1,0:T(8,128)(2,1)S(1)}, bf16[32,512]{1,0:T(8,128)(2,1)S(1)}, u32[]{:S(2)}, u32[]{:S(2)}) collective-permute-start(bf16[32,512]{1,0:T(8,128)(2,1)S(1)} %get-tuple-element.12), channel_id=1, source_target_pairs={{112,128},{240,256},{368,384},{113,129},{241,257},{369,385},{114,1... | collective-permute-start | bytes 98312 | tf_op jit(solution)/shard_map/ppermute | solution.py:529
  2.9 0.7 collective-permute-start.3
  3.6 1.9 %collective-permute-start = (bf16[12,32,256]{2,1,0:T(8,128)(2,1)S(1)}, bf16[12,32,256]{2,1,0:T(8,128)(2,1)S(1)}, u32[]{:S(2)}, u32[]{:S(2)}) collective-permute-start(bf16[12,32,256]{2,1,0:T(8,128)(2,1)S(1)} %get-tuple-element.11), channel_id=1, source_target_pairs={{0,1},{1,2},{2,3},{3,4},{4,5},{5,6},{6,7},{7,8},{8,9},{9,10},{10,1... | collective-permute-start | bytes 589832 | tf_op jit(solution)/shard_map/ppermute | solution.py:528
  5.4 0.2 convert_reduce_fusion
  5.6 0.0 copy-done.9
  5.6 0.0 copy-done.11
  5.7 0.0 copy-start.3
  5.7 1.0 %blur_across.1.across_ref = bf16[12,256,256]{2,1,0:T(8,128)(2,1)S(1)} custom-call(bf16[96,32,512]{2,1,0:T(8,128)(2,1)S(1)} %copy-done, bf16[512,256]{1,0:T(8,128)(2,1)S(1)} %copy-done.1), custom_call_target="tpu_custom_call" | custom-call | flops 805306368 | bytes 4718592 | tf_op jit(solution)/shard_map/blur_across/pallas_call | solution.py:197
  6.7 0.0 copy-start.8
  6.7 0.0 copy-start.6
  6.7 1.3 %collective-permute-done.halo_ref = bf16[12,32,256]{2,1,0:T(8,128)(2,1)S(1)} collective-permute-done((bf16[12,32,256]{2,1,0:T(8,128)(2,1)S(1)}, bf16[12,32,256]{2,1,0:T(8,128)(2,1)S(1)}, u32[]{:S(2)}, u32[]{:S(2)}) %collective-permute-start) | collective-permute-done | bytes 196640 | tf_op jit(solution)/shard_map/ppermute | solution.py:528
  8.1 0.0 copy-done.2
  8.1 0.1 last_planar.1
  8.2 0.0 copy-start.5
  8.2 0.0 copy-start.7
  8.2 5.3 %collective-permute-start.1 = (bf16[16,256]{1,0:T(8,128)(2,1)S(1)}, bf16[16,256]{1,0:T(8,128)(2,1)S(1)}, u32[]{:S(2)}, u32[]{:S(2)}) collective-permute-start(bf16[16,256]{1,0:T(8,128)(2,1)S(1)} %last_planar.1), channel_id=1, source_target_pairs={{0,16},{16,32},{32,48},{48,64},{64,80},{80,96},{96,112},{128,144},... | collective-permute-start | bytes 24584 | tf_op jit(solution)/shard_map/ppermute | solution.py:535
  13.6 0.0 copy-done.3
  13.6 0.8 %row_spectra.1 = (bf16[256,768]{1,0:T(8,128)(2,1)S(1)}, bf16[17,16,256]{2,1,0:T(8,128)(2,1)S(1)}) custom-call(s32[1]{0:T(128)} %bitcast.tile_ref, bf16[12,256,256]{2,1,0:T(8,128)(2,1)S(1)} %blur_across.1.across_ref, bf16[12,32,256]{2,1,0:T(8,128)(2,1)S(1)} %collective-permute-done.halo_ref, bf16[2,128,288]{2,1,0:T(8,128)(2,1)S(1)} %copy-done.2, ...), custom_call_target="tpu_custom_call" | custom-call | flops 226492416 | bytes 1572864 | tf_op jit(solution)/shard_map/row_spectra/pallas_call | solution.py:264
  14.4 0.0 collective-permute-done.2.behind_ref
  14.4 0.0 collective-permute-done.3.corner_ref
  14.4 0.0 collective-permute-done.1.next_ref
  14.4 0.0 copy-done.8
  14.4 0.6 head_spectra.1
  15.0 24.7 %all_to_all.10.spectra_ref = bf16[16,16,768]{2,1,0:T(8,128)(2,1)S(1)} all-to-all(bf16[16,16,768]{2,1,0:T(8,128)(2,1)S(1)} %bitcast.16), channel_id=1, replica_groups=mesh['plane'=32,'tile'=16] {'tile'}, dimensions={0} | all-to-all | bytes 786432 | tf_op jit(solution)/shard_map/all_to_all | solution.py:542
  39.7 0.0 copy-done.6
  39.7 2.0 %cross_spectra.1 = bf16[192,16,128]{2,1,0:T(8,128)(2,1)S(1)} custom-call(s32[1]{0:T(128)} %bitcast.tile_ref, s32[6,64]{1,0:T(8,128)S(1)} %pad_add_fusion.meta_ref, bf16[16,16,768]{2,1,0:T(8,128)(2,1)S(1)} %all_to_all.10.spectra_ref, bf16[128,256]{1,0:T(8,128)(2,1)S(1)} %copy-done.6), custom_call_target="tpu_custom_call" | custom-call | tf_op jit(solution)/shard_map/cross_spectra/pallas_call | solution.py:402
  41.7 25.5 %all_to_all.11 = bf16[16,192,128]{2,1,0:T(8,128)(2,1)S(1)} all-to-all(bf16[16,192,128]{2,1,0:T(8,128)(2,1)S(1)} %bitcast.15), channel_id=1, replica_groups=mesh['plane'=32,'tile'=16] {'tile'}, dimensions={0} | all-to-all | bytes 1572864 | tf_op jit(solution)/shard_map/all_to_all | solution.py:550
  67.2 2.0 %surfaces.1 = bf16[12,128,256]{2,1,0:T(8,128)(2,1)} custom-call(bf16[16,12,16,128]{3,2,1,0:T(8,128)(2,1)S(1)} %bitcast.14, bf16[128,128]{1,0:T(8,128)(2,1)S(1)} %copy-done.7, bf16[256,128]{1,0:T(8,128)(2,1)S(1)} %copy-done.5, bf16[256,256]{1,0:T(8,128)(2,1)S(1)} %copy-done.4), custom_call_target="tpu_custom_call" | custom-call | tf_op jit(solution)/shard_map/surfaces/pallas_call | solution.py:497
  (15 shorter events, 0.0 us)
Async XLA Ops:
  0.0 5.7 %copy-start.1 = (bf16[512,256]{1,0:T(8,128)(2,1)S(1)}, bf16[512,256]{1,0:T(8,128)(2,1)}, u32[]{:S(2)}) copy-start(bf16[512,256]{1,0:T(8,128)(2,1)} %constant.31.clone.table_ref.table_hbm.blur_ref) | copy-start | bytes 786436
  0.0 5.7 %copy-start = (bf16[96,32,512]{2,1,0:T(8,128)(2,1)S(1)}, bf16[96,32,512]{2,1,0:T(8,128)(2,1)}, u32[]{:S(2)}) copy-start(bf16[96,32,512]{2,1,0:T(8,128)(2,1)} %raw_ref.3) | copy-start | bytes 9437188
  0.0 5.4 %copy-start.10 = (s32[64,2]{0,1:T(2,128)S(1)}, s32[64,2]{0,1:T(2,128)}, u32[]{:S(2)}) copy-start(s32[64,2]{0,1:T(2,128)} %param.18) | copy-start | bytes 1540
  0.0 5.4 %copy-start.12 = (s32[64,1]{0,1:T(1,128)S(1)}, s32[64,1]{0,1:T(1,128)}, u32[]{:S(2)}) copy-start(s32[64,1]{0,1:T(1,128)} %param.20) | copy-start | bytes 772
  0.0 5.6 %copy-start.9 = (s32[64,2]{0,1:T(2,128)S(1)}, s32[64,2]{0,1:T(2,128)}, u32[]{:S(2)}) copy-start(s32[64,2]{0,1:T(2,128)} %param.17) | copy-start | bytes 1540
  0.0 5.6 %copy-start.11 = (s32[64]{0:T(128)S(1)}, s32[64]{0:T(128)}, u32[]{:S(2)}) copy-start(s32[64]{0:T(128)} %param.19) | copy-start | bytes 772
  2.1 6.0 %copy-start.2 = (bf16[2,128,288]{2,1,0:T(8,128)(2,1)S(1)}, bf16[2,128,288]{2,1,0:T(8,128)(2,1)}, u32[]{:S(2)}) copy-start(bf16[2,128,288]{2,1,0:T(8,128)(2,1)} %constant.32.clone.grouped_ref) | copy-start | bytes 442372
  2.1 12.3 %collective-permute-start.2 = (bf16[32,512]{1,0:T(8,128)(2,1)S(1)}, bf16[32,512]{1,0:T(8,128)(2,1)S(1)}, u32[]{:S(2)}, u32[]{:S(2)}) collective-permute-start(bf16[32,512]{1,0:T(8,128)(2,1)S(1)} %get-tuple-element.12), channel_id=1, source_target_pairs={{112,128},{240,256},{368,384},{113,129},{241,257},{369,385},{114,1... | collective-permute-start | bytes 98312 | tf_op jit(solution)/shard_map/ppermute | solution.py:529
  2.9 11.5 %collective-permute-start.3 = (bf16[32,512]{1,0:T(8,128)(2,1)S(1)}, bf16[32,512]{1,0:T(8,128)(2,1)S(1)}, u32[]{:S(2)}, u32[]{:S(2)}) collective-permute-start(bf16[32,512]{1,0:T(8,128)(2,1)S(1)} %get-tuple-element.12), channel_id=1, source_target_pairs={{112,129},{113,130},{114,131},{115,132},{116,133},{117,134},{118,1... | collective-permute-start | bytes 98312 | tf_op jit(solution)/shard_map/ppermute | solution.py:530
  3.6 4.5 %collective-permute-start = (bf16[12,32,256]{2,1,0:T(8,128)(2,1)S(1)}, bf16[12,32,256]{2,1,0:T(8,128)(2,1)S(1)}, u32[]{:S(2)}, u32[]{:S(2)}) collective-permute-start(bf16[12,32,256]{2,1,0:T(8,128)(2,1)S(1)} %get-tuple-element.11), channel_id=1, source_target_pairs={{0,1},{1,2},{2,3},{3,4},{4,5},{5,6},{6,7},{7,8},{8,9},{9,10},{10,1... | collective-permute-start | bytes 589832 | tf_op jit(solution)/shard_map/ppermute | solution.py:528
  5.7 7.9 %copy-start.3 = (bf16[256,256]{1,0:T(8,128)(2,1)S(1)}, bf16[256,256]{1,0:T(8,128)(2,1)}, u32[]{:S(2)}) copy-start(bf16[256,256]{1,0:T(8,128)(2,1)} %constant.33.clone.table_ref) | copy-start | bytes 393220
  6.7 7.7 %copy-start.8 = (bf16[2,16,40]{2,1,0:T(8,128)(2,1)S(1)}, bf16[2,16,40]{2,1,0:T(8,128)(2,1)}, u32[]{:S(2)}) copy-start(bf16[2,16,40]{2,1,0:T(8,128)(2,1)} %constant.34.clone.single_ref) | copy-start | bytes 7684
  6.7 33.0 %copy-start.6 = (bf16[128,256]{1,0:T(8,128)(2,1)S(1)}, bf16[128,256]{1,0:T(8,128)(2,1)}, u32[]{:S(2)}) copy-start(bf16[128,256]{1,0:T(8,128)(2,1)} %constant.35.clone.table_ref) | copy-start | bytes 196612
  8.2 59.0 %copy-start.4 = (bf16[256,256]{1,0:T(8,128)(2,1)S(1)}, bf16[256,256]{1,0:T(8,128)(2,1)}, u32[]{:S(2)}) copy-start(bf16[256,256]{1,0:T(8,128)(2,1)} %constant.38.clone.row_ref) | copy-start | bytes 393220
  8.2 59.0 %copy-start.5 = (bf16[256,128]{1,0:T(8,128)(2,1)S(1)}, bf16[256,128]{1,0:T(8,128)(2,1)}, u32[]{:S(2)}) copy-start(bf16[256,128]{1,0:T(8,128)(2,1)} %constant.37.clone.column_ref) | copy-start | bytes 196612
  8.2 59.0 %copy-start.7 = (bf16[128,128]{1,0:T(8,128)(2,1)S(1)}, bf16[128,128]{1,0:T(8,128)(2,1)}, u32[]{:S(2)}) copy-start(bf16[128,128]{1,0:T(8,128)(2,1)} %constant.36.clone.reversal_ref) | copy-start | bytes 98308
  8.2 6.2 %collective-permute-start.1 = (bf16[16,256]{1,0:T(8,128)(2,1)S(1)}, bf16[16,256]{1,0:T(8,128)(2,1)S(1)}, u32[]{:S(2)}, u32[]{:S(2)}) collective-permute-start(bf16[16,256]{1,0:T(8,128)(2,1)S(1)} %last_planar.1), channel_id=1, source_target_pairs={{0,16},{16,32},{32,48},{48,64},{64,80},{80,96},{96,112},{128,144},... | collective-permute-start | bytes 24584 | tf_op jit(solution)/shard_map/ppermute | solution.py:535

commit v2 on v1

--- a/solution.py
+++ b/solution.py
@@ -14,6 +14,7 @@
 HALF = 256
 TILES = 16
 DEPTH = 8
+HALO = 3
 FREQS = 8
 GROUP = 8
 VMEM_LIMIT = 24 * 1024 * 1024
@@ -52,32 +53,33 @@
     )
 
 
-def column_weights(first_tile):
+def column_weights(last_tile):
     local = np.zeros((16, 32), np.float32)
-    halo = np.zeros((16, 4), np.float32)
+    halo = np.zeros((16, HALO), np.float32)
     for i in range(16):
         for c in range(32):
-            local[i, c] = blur_weight(c + 2 - 2 * i)
-        for h in range(4):
-            halo[i, h] = blur_weight(h - 2 - 2 * i)
-    if first_tile:
-        local[0, 0] = 0.0
-        halo[1, :] = 0.0
+            local[i, c] = blur_weight(c - 2 - 2 * i)
+        for h in range(HALO):
+            halo[i, h] = blur_weight(30 + h - 2 * i)
+    if last_tile:
+        halo[14, :] = 0.0
+        local[15, :] = 0.0
     return local, halo
 
 
 def column_tables():
-    grouped = np.zeros((2, GROUP * 16, GROUP * 36), np.float32)
+    width = 32 + HALO
+    grouped = np.zeros((2, GROUP * 16, GROUP * width), np.float32)
     single = np.zeros((2, 16, 40), np.float32)
     for variant in (0, 1):
-        local, halo = column_weights(variant == 0)
+        local, halo = column_weights(variant == 1)
         for q in range(GROUP):
             rows = slice(q * 16, q * 16 + 16)
             grouped[variant, rows, q * 32 : q * 32 + 32] = local
-            at = GROUP * 32 + q * 4
-            grouped[variant, rows, at : at + 4] = halo
+            at = GROUP * 32 + q * HALO
+            grouped[variant, rows, at : at + HALO] = halo
         single[variant, :, :32] = local
-        single[variant, :, 36:40] = halo
+        single[variant, :, 32 : 32 + HALO] = halo
     return grouped.astype(jnp.bfloat16), single.astype(jnp.bfloat16)
 
 
@@ -124,7 +126,7 @@
     )
 
 
-def edge_kernel(raw_ref, table_hbm, edge_ref, last_ref, strip_ref, table_ref, sems):
+def edge_kernel(raw_ref, table_hbm, edge_ref, strip_ref, table_ref, sems):
     planes = raw_ref.shape[0]
     part = 32
     copies = []
@@ -132,29 +134,26 @@
         held = pl.ds(k * part, part)
         copies.append(
             pltpu.make_async_copy(
-                raw_ref.at[held, pl.ds(24, 8), :], strip_ref.at[held], sems.at[k]
+                raw_ref.at[held, pl.ds(0, 8), :], strip_ref.at[held], sems.at[k]
             )
         )
     copies.insert(1, pltpu.make_async_copy(table_hbm, table_ref, sems.at[planes // part]))
-    copies.append(
-        pltpu.make_async_copy(raw_ref.at[planes - 1], last_ref, sems.at[planes // part + 1])
-    )
     for copy in copies:
         copy.start()
-    upper = lax.broadcasted_iota(jnp.int32, (8, HALF), 0) < 4
+    shape = (part * HALO, part * 8)
+    row = lax.broadcasted_iota(jnp.int32, shape, 0)
+    source = lax.broadcasted_iota(jnp.int32, shape, 1)
+    wanted = (source >> 3) * HALO + (source & 7)
+    select = jnp.where((row == wanted) & ((source & 7) < HALO), 1.0, 0.0)
+    select = select.astype(jnp.bfloat16)
     per = part // GROUP
     copies.pop(1).wait()
     for k in range(planes // part):
         copies[k].wait()
         cells = strip_ref[k * part : (k + 1) * part].reshape(part * 8, FACE)
-        across = dot(cells, table_ref[...])
-        edges = []
-        for q in range(0, part * 8, 16):
-            turned = pltpu.roll(across[q : q + 8], 4, 0)
-            edges.append(jnp.where(upper, turned, across[q + 8 : q + 16]))
-        edges = jnp.concatenate(edges, axis=0).astype(jnp.bfloat16)
-        edge_ref[k * per : (k + 1) * per] = edges.reshape(per, GROUP * 4, HALF)
-    copies[-1].wait()
+        across = dot(cells, table_ref[...]).astype(jnp.bfloat16)
+        edges = dot(select, across).astype(jnp.bfloat16)
+        edge_ref[k * per : (k + 1) * per] = edges.reshape(per, GROUP * HALO, HALF)
 
 
 def blur_edges(raw, table):
@@ -162,15 +161,14 @@
     return pl.pallas_call(
         edge_kernel,
         in_specs=[whole(pltpu.HBM)] * 2,
-        out_specs=[whole()] * 2,
-        out_shape=[
-            jax.ShapeDtypeStruct((planes // GROUP, GROUP * 4, HALF), jnp.bfloat16),
-            jax.ShapeDtypeStruct((32, FACE), jnp.bfloat16),
-        ],
+        out_specs=whole(),
+        out_shape=jax.ShapeDtypeStruct(
+            (planes // GROUP, GROUP * HALO, HALF), jnp.bfloat16
+        ),
         scratch_shapes=[
             pltpu.VMEM((planes, 8, FACE), jnp.bfloat16),
             pltpu.VMEM((FACE, HALF), jnp.bfloat16),
-            pltpu.SemaphoreType.DMA((planes // 32 + 2,)),
+            pltpu.SemaphoreType.DMA((planes // 32 + 1,)),
         ],
         compiler_params=params(),
         cost_estimate=pl.CostEstimate(
@@ -212,7 +210,7 @@
 def last_kernel(tile_ref, across_ref, halo_ref, grouped_ref, out_ref):
     last = across_ref.shape[0] - 1
     stacked = jnp.concatenate([across_ref[last], halo_ref[last]], axis=0)
-    weights = grouped_ref[jnp.minimum(tile_ref[0], 1), (GROUP - 1) * 16 :]
+    weights = grouped_ref[jnp.where(tile_ref[0] == TILES - 1, 1, 0), (GROUP - 1) * 16 :]
     out_ref[...] = dot(weights, stacked).astype(jnp.bfloat16)
 
 
@@ -236,7 +234,7 @@
     tile_ref, across_ref, halo_ref, grouped_ref, table_ref, out_ref, head_ref, planar_ref
 ):
     groups = across_ref.shape[0]
-    weights = grouped_ref[jnp.minimum(tile_ref[0], 1)]
+    weights = grouped_ref[jnp.where(tile_ref[0] == TILES - 1, 1, 0)]
     for g in range(groups):
         stacked = jnp.concatenate([across_ref[g], halo_ref[g]], axis=0)
         planar = dot(weights, stacked).astype(jnp.bfloat16)
@@ -284,9 +282,9 @@
     tile_ref, slab_ref, next_ref, behind_ref, corner_ref, blur_ref, single_ref,
     head_ref, table_ref, spectra_ref, out_ref,
 ):
-    rows = jnp.concatenate([behind_ref[...], corner_ref[24:]], axis=0)
+    rows = jnp.concatenate([behind_ref[...], corner_ref[:8]], axis=0)
     rows = dot(rows, blur_ref[...]).astype(jnp.bfloat16)
-    weights = single_ref[jnp.minimum(tile_ref[0], 1)]
+    weights = single_ref[jnp.where(tile_ref[0] == TILES - 1, 1, 0)]
     far = dot(weights, rows)
     wrapped = lax.rem(slab_ref[0], DEPTH) == 0
     before = jnp.where(wrapped, far, next_ref[...].astype(jnp.float32))
@@ -347,7 +345,7 @@
             for side in range(2):
                 which = meta_ref[side, n]
                 start = meta_ref[2 + side, n]
-                from_low = (lane >= start) | (lane < start - 128)
+                from_low = (lane >= start) & (lane < start + 128)
                 mixed = jnp.where(from_low, held_ref[which, 0], held_ref[which, 1])
                 turned = pltpu.roll(mixed, (256 - start) & 127, 1)
                 band = jnp.where(live, turned, 0.0)
@@ -394,7 +392,7 @@
     earlier = (owners[:, None] == owners[None, :]) & (position[None, :] < position[:, None])
     slots = jnp.sum(earlier.astype(jnp.int32), axis=1)
     places = owners * OWN_CAP + slots
-    return jnp.concatenate([sections.T, rows.T + 1, extents[None], places[None]], axis=0)
+    return jnp.concatenate([sections.T, rows.T - 1, extents[None], places[None]], axis=0)
 
 
 def cross_spectra(tile, meta, spectra, table):
@@ -520,11 +518,12 @@
 
     far = [s for s in range(slabs - 1) if (s + 1) % DEPTH == 0]
     near = [s for s in range(slabs - 1) if (s + 1) % DEPTH]
-    turns = [(t, (t + 1) % TILES) for t in range(TILES)]
+    turns = [((t + 1) % TILES, t) for t in range(TILES)]
     corners = [(s * TILES + t, (s + 1) * TILES + u) for s in far for t, u in turns]
     table = pltpu.with_memory_space_constraint(jnp.asarray(blur_matrix()), pltpu.HBM)
     held = pltpu.with_memory_space_constraint(raw_planes, pltpu.HBM)
-    edges, last = blur_edges(held, table)
+    edges = blur_edges(held, table)
+    last = raw_planes[raw_planes.shape[0] - 1]
     halo = lax.ppermute(edges, "tile", turns)
     behind = lax.ppermute(last, "plane", [(s, s + 1) for s in far])
     corner = lax.ppermute(last, ("plane", "tile"), corners)

time: 69.4 us -> 67.5 us (0.973)
  the two profiles are of different devices: /device:TPU:199 before, /device:TPU:7 now
where the time goes in v2:
time: 67.5 us; the launch traced here: 66.5 us
  blocking collectives  46.1 us (68%)
  Pallas kernels  8.75 us (13%)
  starting transfers between devices  6.26 us (9%)
  waiting for transfers between devices  4 us (6%)
  local copies, waits for them, and re-layouts  1 us (1%)
    all_to_all x1, blocking collectives, correlate(): lax.all_to_all(cross.reshape(TILES, OWN_CAP * 16, 128), 'tile', 0, 0, til...  25.5 us
    all_to_all x1, blocking collectives, correlate(): lax.all_to_all(spectra.reshape(TILES, 16, spectra.shape[1]), 'tile', 0, 0...  20.6 us
    ppermute x1, starting transfers between devices, correlate(): last = lax.ppermute(last, 'plane', [(s, s + 1) for s in near])  2.87 us
    ppermute x1, waiting for transfers between devices, correlate(): halo = lax.ppermute(edges, 'tile', turns)  2.73 us
    pallas_call x1, Pallas kernels, blur_edges(): pl.pallas_call(edge_kernel, in_specs=[whole(pltpu.HBM)] * 2, out_specs=wh...  2.34 us
    pallas_call x1, Pallas kernels, surfaces(): pl.pallas_call(surface_kernel, in_specs=[whole()] * 4, out_specs=whole(pl...  2 us
    pallas_call x1, Pallas kernels, cross_spectra(): pl.pallas_call(cross_kernel, in_specs=[whole(pltpu.SMEM)] * 2 + [whole()]...  1.99 us
    ppermute x1, starting transfers between devices, correlate(): behind = lax.ppermute(last, 'plane', [(s, s + 1) for s in far])  1.41 us
  transfers between devices with their start and end apart: 4, of which 2 were waited for; matrix products, arithmetic and copies ran while one was open for 0% of the time, Pallas kernels for 6%

profile of v2, /device:TPU:7, one launch (start us, length us, event | category | flops | bytes accessed | tf_op | source)
XLA Modules:
  0.0 66.5 jit_solution(6615539990309695926)
XLA Ops:
  0.0 0.0 copy-start.12
  0.0 0.0 copy-start.9
  0.0 0.0 copy-start.11
  0.0 0.9 %slice_bitcast_fusion = bf16[32,512]{1,0:T(8,128)(2,1)S(1)} fusion(bf16[96,32,512]{2,1,0:T(8,128)(2,1)} %raw_ref.3), kind=kLoop, calls=%fused_computation.2 | loop fusion | bytes 65536 | tf_op jit(solution)/shard_map/squeeze | solution.py:526
  1.0 1.4 %collective-permute-start.2 = (bf16[32,512]{1,0:T(8,128)(2,1)S(1)}, bf16[32,512]{1,0:T(8,128)(2,1)S(1)}, u32[]{:S(2)}, u32[]{:S(2)}) collective-permute-start(bf16[32,512]{1,0:T(8,128)(2,1)S(1)} %slice_bitcast_fusion), channel_id=1, source_target_pairs={{112,128},{240,256},{368,384},{113,129},{241,257},{369,385},{114,1... | collective-permute-start | bytes 98312 | tf_op jit(solution)/shard_map/ppermute | solution.py:528
  2.4 1.3 %collective-permute-start.3 = (bf16[32,512]{1,0:T(8,128)(2,1)S(1)}, bf16[32,512]{1,0:T(8,128)(2,1)S(1)}, u32[]{:S(2)}, u32[]{:S(2)}) collective-permute-start(bf16[32,512]{1,0:T(8,128)(2,1)S(1)} %slice_bitcast_fusion), channel_id=1, source_target_pairs={{113,128},{114,129},{115,130},{116,131},{117,132},{118,133},{119,1... | collective-permute-start | bytes 98312 | tf_op jit(solution)/shard_map/ppermute | solution.py:529
  3.7 2.3 %blur_edges.1 = bf16[12,24,256]{2,1,0:T(8,128)(2,1)S(1)} custom-call(bf16[96,32,512]{2,1,0:T(8,128)(2,1)} %raw_ref.3, bf16[512,256]{1,0:T(8,128)(2,1)} %constant.32.clone.table_ref.table_hbm.blur_ref), custom_call_target="tpu_custom_call" | custom-call | flops 201326592 | bytes 786432 | tf_op jit(solution)/shard_map/blur_edges/pallas_call | solution.py:161
  6.0 0.0 copy-start.2
  6.0 0.7 %collective-permute-start = (bf16[12,24,256]{2,1,0:T(8,128)(2,1)S(1)}, bf16[12,24,256]{2,1,0:T(8,128)(2,1)S(1)}, u32[]{:S(2)}, u32[]{:S(2)}) collective-permute-start(bf16[12,24,256]{2,1,0:T(8,128)(2,1)S(1)} %blur_edges.1), channel_id=1, source_target_pairs={{1,0},{2,1},{3,2},{4,3},{5,4},{6,5},{7,6},{8,7},{9,8},{10,9},{11,1... | collective-permute-start | bytes 442376 | tf_op jit(solution)/shard_map/ppermute | solution.py:527
  6.7 0.0 copy-done.10
  6.7 0.0 copy-done.12
  6.7 0.2 convert_reduce_fusion
  6.9 0.0 copy-done.9
  7.0 0.0 copy-start.3
  7.0 1.0 %blur_across.1.across_ref = bf16[12,256,256]{2,1,0:T(8,128)(2,1)S(1)} custom-call(bf16[96,32,512]{2,1,0:T(8,128)(2,1)S(1)} %copy-done, bf16[512,256]{1,0:T(8,128)(2,1)S(1)} %copy-done.1), custom_call_target="tpu_custom_call" | custom-call | flops 805306368 | bytes 4718592 | tf_op jit(solution)/shard_map/blur_across/pallas_call | solution.py:195
  8.0 0.0 copy-start.8
  8.0 0.0 copy-start.6
  8.0 2.7 %collective-permute-done.halo_ref = bf16[12,24,256]{2,1,0:T(8,128)(2,1)S(1)} collective-permute-done((bf16[12,24,256]{2,1,0:T(8,128)(2,1)S(1)}, bf16[12,24,256]{2,1,0:T(8,128)(2,1)S(1)}, u32[]{:S(2)}, u32[]{:S(2)}) %collective-permute-start) | collective-permute-done | bytes 147488 | tf_op jit(solution)/shard_map/ppermute | solution.py:527
  10.7 0.1 last_planar.1
  10.8 0.0 copy-start.5
  10.9 0.0 copy-start.7
  10.9 2.9 %collective-permute-start.1 = (bf16[16,256]{1,0:T(8,128)(2,1)S(1)}, bf16[16,256]{1,0:T(8,128)(2,1)S(1)}, u32[]{:S(2)}, u32[]{:S(2)}) collective-permute-start(bf16[16,256]{1,0:T(8,128)(2,1)S(1)} %last_planar.1), channel_id=1, source_target_pairs={{0,16},{16,32},{32,48},{48,64},{64,80},{80,96},{96,112},{128,144},... | collective-permute-start | bytes 24584 | tf_op jit(solution)/shard_map/ppermute | solution.py:534
  13.8 0.0 copy-done.3
  13.8 0.8 %row_spectra.1 = (bf16[256,768]{1,0:T(8,128)(2,1)S(1)}, bf16[17,16,256]{2,1,0:T(8,128)(2,1)S(1)}) custom-call(s32[1]{0:T(128)} %bitcast.tile_ref, bf16[12,256,256]{2,1,0:T(8,128)(2,1)S(1)} %blur_across.1.across_ref, bf16[12,24,256]{2,1,0:T(8,128)(2,1)S(1)} %collective-permute-done.halo_ref, bf16[2,128,280]{2,1,0:T(8,128)(2,1)S(1)} %copy-done.2, ...), custom_call_target="tpu_custom_call" | custom-call | flops 226492416 | bytes 1572864 | tf_op jit(solution)/shard_map/row_spectra/pallas_call | solution.py:262
  14.6 0.0 collective-permute-done.2.behind_ref
  14.6 1.3 %collective-permute-done.3.corner_ref = bf16[32,512]{1,0:T(8,128)(2,1)S(1)} collective-permute-done((bf16[32,512]{1,0:T(8,128)(2,1)S(1)}, bf16[32,512]{1,0:T(8,128)(2,1)S(1)}, u32[]{:S(2)}, u32[]{:S(2)}) %collective-permute-start.3) | collective-permute-done | bytes 32800 | tf_op jit(solution)/shard_map/ppermute | solution.py:529
  15.8 0.0 collective-permute-done.1.next_ref
  15.8 0.6 head_spectra.1
  16.4 20.6 %all_to_all.10.spectra_ref = bf16[16,16,768]{2,1,0:T(8,128)(2,1)S(1)} all-to-all(bf16[16,16,768]{2,1,0:T(8,128)(2,1)S(1)} %bitcast.18), channel_id=1, replica_groups=mesh['plane'=32,'tile'=16] {'tile'}, dimensions={0} | all-to-all | bytes 786432 | tf_op jit(solution)/shard_map/all_to_all | solution.py:541
  37.0 2.0 %cross_spectra.1 = bf16[192,16,128]{2,1,0:T(8,128)(2,1)S(1)} custom-call(s32[1]{0:T(128)} %bitcast.tile_ref, s32[6,64]{1,0:T(8,128)S(1)} %pad_add_fusion.meta_ref, bf16[16,16,768]{2,1,0:T(8,128)(2,1)S(1)} %all_to_all.10.spectra_ref, bf16[128,256]{1,0:T(8,128)(2,1)S(1)} %copy-done.6), custom_call_target="tpu_custom_call" | custom-call | tf_op jit(solution)/shard_map/cross_spectra/pallas_call | solution.py:400
  39.0 25.5 %all_to_all.11 = bf16[16,192,128]{2,1,0:T(8,128)(2,1)S(1)} all-to-all(bf16[16,192,128]{2,1,0:T(8,128)(2,1)S(1)} %bitcast.17), channel_id=1, replica_groups=mesh['plane'=32,'tile'=16] {'tile'}, dimensions={0} | all-to-all | bytes 1572864 | tf_op jit(solution)/shard_map/all_to_all | solution.py:549
  64.5 2.0 %surfaces.1 = bf16[12,128,256]{2,1,0:T(8,128)(2,1)} custom-call(bf16[16,12,16,128]{3,2,1,0:T(8,128)(2,1)S(1)} %bitcast.16, bf16[128,128]{1,0:T(8,128)(2,1)S(1)} %copy-done.7, bf16[256,128]{1,0:T(8,128)(2,1)S(1)} %copy-done.5, bf16[256,256]{1,0:T(8,128)(2,1)S(1)} %copy-done.4), custom_call_target="tpu_custom_call" | custom-call | tf_op jit(solution)/shard_map/surfaces/pallas_call | solution.py:495
  (16 shorter events, 0.0 us)
Async XLA Ops:
  0.0 7.0 %copy-start.1 = (bf16[512,256]{1,0:T(8,128)(2,1)S(1)}, bf16[512,256]{1,0:T(8,128)(2,1)}, u32[]{:S(2)}) copy-start(bf16[512,256]{1,0:T(8,128)(2,1)} %constant.32.clone.table_ref.table_hbm.blur_ref) | copy-start | bytes 786436
  0.0 7.0 %copy-start = (bf16[96,32,512]{2,1,0:T(8,128)(2,1)S(1)}, bf16[96,32,512]{2,1,0:T(8,128)(2,1)}, u32[]{:S(2)}) copy-start(bf16[96,32,512]{2,1,0:T(8,128)(2,1)} %raw_ref.3) | copy-start | bytes 9437188
  0.0 6.7 %copy-start.10 = (s32[64,2]{0,1:T(2,128)S(1)}, s32[64,2]{0,1:T(2,128)}, u32[]{:S(2)}) copy-start(s32[64,2]{0,1:T(2,128)} %param.18) | copy-start | bytes 1540
  0.0 6.7 %copy-start.12 = (s32[64,1]{0,1:T(1,128)S(1)}, s32[64,1]{0,1:T(1,128)}, u32[]{:S(2)}) copy-start(s32[64,1]{0,1:T(1,128)} %param.20) | copy-start | bytes 772
  0.0 6.9 %copy-start.9 = (s32[64,2]{0,1:T(2,128)S(1)}, s32[64,2]{0,1:T(2,128)}, u32[]{:S(2)}) copy-start(s32[64,2]{0,1:T(2,128)} %param.17) | copy-start | bytes 1540
  0.0 6.9 %copy-start.11 = (s32[64]{0:T(128)S(1)}, s32[64]{0:T(128)}, u32[]{:S(2)}) copy-start(s32[64]{0:T(128)} %param.19) | copy-start | bytes 772
  1.0 13.6 %collective-permute-start.2 = (bf16[32,512]{1,0:T(8,128)(2,1)S(1)}, bf16[32,512]{1,0:T(8,128)(2,1)S(1)}, u32[]{:S(2)}, u32[]{:S(2)}) collective-permute-start(bf16[32,512]{1,0:T(8,128)(2,1)S(1)} %slice_bitcast_fusion), channel_id=1, source_target_pairs={{112,128},{240,256},{368,384},{113,129},{241,257},{369,385},{114,1... | collective-permute-start | bytes 98312 | tf_op jit(solution)/shard_map/ppermute | solution.py:528
  2.4 13.5 %collective-permute-start.3 = (bf16[32,512]{1,0:T(8,128)(2,1)S(1)}, bf16[32,512]{1,0:T(8,128)(2,1)S(1)}, u32[]{:S(2)}, u32[]{:S(2)}) collective-permute-start(bf16[32,512]{1,0:T(8,128)(2,1)S(1)} %slice_bitcast_fusion), channel_id=1, source_target_pairs={{113,128},{114,129},{115,130},{116,131},{117,132},{118,133},{119,1... | collective-permute-start | bytes 98312 | tf_op jit(solution)/shard_map/ppermute | solution.py:529
  6.0 4.7 %copy-start.2 = (bf16[2,128,280]{2,1,0:T(8,128)(2,1)S(1)}, bf16[2,128,280]{2,1,0:T(8,128)(2,1)}, u32[]{:S(2)}) copy-start(bf16[2,128,280]{2,1,0:T(8,128)(2,1)} %constant.33.clone.grouped_ref) | copy-start | bytes 430084
  6.0 4.7 %collective-permute-start = (bf16[12,24,256]{2,1,0:T(8,128)(2,1)S(1)}, bf16[12,24,256]{2,1,0:T(8,128)(2,1)S(1)}, u32[]{:S(2)}, u32[]{:S(2)}) collective-permute-start(bf16[12,24,256]{2,1,0:T(8,128)(2,1)S(1)} %blur_edges.1), channel_id=1, source_target_pairs={{1,0},{2,1},{3,2},{4,3},{5,4},{6,5},{7,6},{8,7},{9,8},{10,9},{11,1... | collective-permute-start | bytes 442376 | tf_op jit(solution)/shard_map/ppermute | solution.py:527
  7.0 6.8 %copy-start.3 = (bf16[256,256]{1,0:T(8,128)(2,1)S(1)}, bf16[256,256]{1,0:T(8,128)(2,1)}, u32[]{:S(2)}) copy-start(bf16[256,256]{1,0:T(8,128)(2,1)} %constant.34.clone.table_ref) | copy-start | bytes 393220
  8.0 7.9 %copy-start.8 = (bf16[2,16,40]{2,1,0:T(8,128)(2,1)S(1)}, bf16[2,16,40]{2,1,0:T(8,128)(2,1)}, u32[]{:S(2)}) copy-start(bf16[2,16,40]{2,1,0:T(8,128)(2,1)} %constant.35.clone.single_ref) | copy-start | bytes 7684
  8.0 29.1 %copy-start.6 = (bf16[128,256]{1,0:T(8,128)(2,1)S(1)}, bf16[128,256]{1,0:T(8,128)(2,1)}, u32[]{:S(2)}) copy-start(bf16[128,256]{1,0:T(8,128)(2,1)} %constant.36.clone.table_ref) | copy-start | bytes 196612
  10.8 53.7 %copy-start.4 = (bf16[256,256]{1,0:T(8,128)(2,1)S(1)}, bf16[256,256]{1,0:T(8,128)(2,1)}, u32[]{:S(2)}) copy-start(bf16[256,256]{1,0:T(8,128)(2,1)} %constant.39.clone.row_ref) | copy-start | bytes 393220
  10.8 53.7 %copy-start.5 = (bf16[256,128]{1,0:T(8,128)(2,1)S(1)}, bf16[256,128]{1,0:T(8,128)(2,1)}, u32[]{:S(2)}) copy-start(bf16[256,128]{1,0:T(8,128)(2,1)} %constant.38.clone.column_ref) | copy-start | bytes 196612
  10.9 53.7 %copy-start.7 = (bf16[128,128]{1,0:T(8,128)(2,1)S(1)}, bf16[128,128]{1,0:T(8,128)(2,1)}, u32[]{:S(2)}) copy-start(bf16[128,128]{1,0:T(8,128)(2,1)} %constant.37.clone.reversal_ref) | copy-start | bytes 98308
  10.9 5.0 %collective-permute-start.1 = (bf16[16,256]{1,0:T(8,128)(2,1)S(1)}, bf16[16,256]{1,0:T(8,128)(2,1)S(1)}, u32[]{:S(2)}, u32[]{:S(2)}) collective-permute-start(bf16[16,256]{1,0:T(8,128)(2,1)S(1)} %last_planar.1), channel_id=1, source_target_pairs={{0,16},{16,32},{32,48},{48,64},{64,80},{80,96},{96,112},{128,144},... | collective-permute-start | bytes 24584 | tf_op jit(solution)/shard_map/ppermute | solution.py:534

commit v3 on v2

--- a/solution.py
+++ b/solution.py
@@ -126,77 +126,71 @@
     )
 
 
-def edge_kernel(raw_ref, table_hbm, edge_ref, strip_ref, table_ref, sems):
+def plane_kernel(raw_ref, table_hbm, last_ref, across_ref, edge_ref, table_ref, sems):
     planes = raw_ref.shape[0]
-    part = 32
-    copies = []
-    for k in range(planes // part):
-        held = pl.ds(k * part, part)
-        copies.append(
-            pltpu.make_async_copy(
-                raw_ref.at[held, pl.ds(0, 8), :], strip_ref.at[held], sems.at[k]
-            )
-        )
-    copies.insert(1, pltpu.make_async_copy(table_hbm, table_ref, sems.at[planes // part]))
-    for copy in copies:
-        copy.start()
-    shape = (part * HALO, part * 8)
+    table_copy = pltpu.make_async_copy(table_hbm, table_ref, sems.at[0])
+    plane_copy = pltpu.make_async_copy(raw_ref.at[planes - 1], last_ref, sems.at[1])
+    table_copy.start()
+    plane_copy.start()
+    table_copy.wait()
+    plane_copy.wait()
+    across = dot(last_ref[...], table_ref[...]).astype(jnp.bfloat16)
+    across_ref[...] = across
+    edge_ref[...] = across[:8]
+
+
+def blur_last(raw, table):
+    return pl.pallas_call(
+        plane_kernel,
+        in_specs=[whole(pltpu.HBM)] * 2,
+        out_specs=[whole()] * 3,
+        out_shape=[
+            jax.ShapeDtypeStruct((32, FACE), jnp.bfloat16),
+            jax.ShapeDtypeStruct((32, HALF), jnp.bfloat16),
+            jax.ShapeDtypeStruct((8, HALF), jnp.bfloat16),
+        ],
+        scratch_shapes=[
+            pltpu.VMEM((FACE, HALF), jnp.bfloat16),
+            pltpu.SemaphoreType.DMA((2,)),
+        ],
+        compiler_params=params(),
+        name="blur_last",
+    )(raw, table)
+
+
+def across_kernel(raw_ref, table_ref, across_ref, edge_ref):
+    planes = raw_ref.shape[0]
+    part = 16
+    per = part // GROUP
+    shape = (GROUP * HALO, GROUP * 8)
     row = lax.broadcasted_iota(jnp.int32, shape, 0)
     source = lax.broadcasted_iota(jnp.int32, shape, 1)
     wanted = (source >> 3) * HALO + (source & 7)
     select = jnp.where((row == wanted) & ((source & 7) < HALO), 1.0, 0.0)
     select = select.astype(jnp.bfloat16)
-    per = part // GROUP
-    copies.pop(1).wait()
-    for k in range(planes // part):
-        copies[k].wait()
-        cells = strip_ref[k * part : (k + 1) * part].reshape(part * 8, FACE)
-        across = dot(cells, table_ref[...]).astype(jnp.bfloat16)
-        edges = dot(select, across).astype(jnp.bfloat16)
-        edge_ref[k * per : (k + 1) * per] = edges.reshape(per, GROUP * HALO, HALF)
-
-
-def blur_edges(raw, table):
-    planes = raw.shape[0]
-    return pl.pallas_call(
-        edge_kernel,
-        in_specs=[whole(pltpu.HBM)] * 2,
-        out_specs=whole(),
-        out_shape=jax.ShapeDtypeStruct(
-            (planes // GROUP, GROUP * HALO, HALF), jnp.bfloat16
-        ),
-        scratch_shapes=[
-            pltpu.VMEM((planes, 8, FACE), jnp.bfloat16),
-            pltpu.VMEM((FACE, HALF), jnp.bfloat16),
-            pltpu.SemaphoreType.DMA((planes // 32 + 1,)),
-        ],
-        compiler_params=params(),
-        cost_estimate=pl.CostEstimate(
-            flops=2 * planes * 8 * FACE * HALF,
-            bytes_accessed=planes * 8 * FACE * 2,
-            transcendentals=0,
-        ),
-        name="blur_edges",
-    )(raw, table)
-
-
-def across_kernel(raw_ref, table_ref, across_ref):
-    planes = raw_ref.shape[0]
-    part = 16
-    per = part // GROUP
     for k in range(planes // part):
         cells = raw_ref[k * part : (k + 1) * part].reshape(part * 32, FACE)
-        across = dot(cells, table_ref[...]).astype(jnp.bfloat16)
-        across_ref[k * per : (k + 1) * per] = across.reshape(per, GROUP * 32, HALF)
+        across = dot(cells, table_ref[...])
+        held = across.astype(jnp.bfloat16).reshape(per, GROUP * 32, HALF)
+        across_ref[k * per : (k + 1) * per] = held
+        for g in range(per):
+            at = g * GROUP * 32
+            tops = [across[at + 32 * q : at + 32 * q + 8] for q in range(GROUP)]
+            tops = jnp.concatenate(tops, axis=0).astype(jnp.bfloat16)
+            edge_ref[k * per + g] = dot(select, tops).astype(jnp.bfloat16)
 
 
 def blur_across(raw, table):
     planes = raw.shape[0]
+    groups = planes // GROUP
     return pl.pallas_call(
         across_kernel,
         in_specs=[whole()] * 2,
-        out_specs=whole(),
-        out_shape=jax.ShapeDtypeStruct((planes // GROUP, GROUP * 32, HALF), jnp.bfloat16),
+        out_specs=[whole()] * 2,
+        out_shape=[
+            jax.ShapeDtypeStruct((groups, GROUP * 32, HALF), jnp.bfloat16),
+            jax.ShapeDtypeStruct((groups, GROUP * HALO, HALF), jnp.bfloat16),
+        ],
         compiler_params=params(),
         cost_estimate=pl.CostEstimate(
             flops=2 * planes * 32 * FACE * HALF,
@@ -207,14 +201,13 @@
     )(raw, table)
 
 
-def last_kernel(tile_ref, across_ref, halo_ref, grouped_ref, out_ref):
-    last = across_ref.shape[0] - 1
-    stacked = jnp.concatenate([across_ref[last], halo_ref[last]], axis=0)
-    weights = grouped_ref[jnp.where(tile_ref[0] == TILES - 1, 1, 0), (GROUP - 1) * 16 :]
-    out_ref[...] = dot(weights, stacked).astype(jnp.bfloat16)
-
-
-def last_planar(tile, across, halo, grouped):
+def last_kernel(tile_ref, across_ref, halo_ref, single_ref, out_ref):
+    rows = jnp.concatenate([across_ref[...], halo_ref[...]], axis=0)
+    weights = single_ref[jnp.where(tile_ref[0] == TILES - 1, 1, 0)]
+    out_ref[...] = dot(weights, rows).astype(jnp.bfloat16)
+
+
+def last_planar(tile, across, halo, single):
     return pl.pallas_call(
         last_kernel,
         in_specs=[whole(pltpu.SMEM)] + [whole()] * 3,
@@ -222,7 +215,7 @@
         out_shape=jax.ShapeDtypeStruct((16, HALF), jnp.bfloat16),
         compiler_params=params(),
         name="last_planar",
-    )(tile, across, halo, grouped)
+    )(tile, across, halo, single)
 
 
 def blend(before, middle, after):
@@ -522,16 +515,16 @@
     corners = [(s * TILES + t, (s + 1) * TILES + u) for s in far for t, u in turns]
     table = pltpu.with_memory_space_constraint(jnp.asarray(blur_matrix()), pltpu.HBM)
     held = pltpu.with_memory_space_constraint(raw_planes, pltpu.HBM)
-    edges = blur_edges(held, table)
-    last = raw_planes[raw_planes.shape[0] - 1]
+    grouped, single = column_tables()
+    raw_last, last, edge = blur_last(held, table)
+    corner = lax.ppermute(raw_last, ("plane", "tile"), corners)
+    behind = lax.ppermute(raw_last, "plane", [(s, s + 1) for s in far])
+    edge = lax.ppermute(edge, "tile", turns)
+    across, edges = blur_across(raw_planes, blur_matrix())
     halo = lax.ppermute(edges, "tile", turns)
-    behind = lax.ppermute(last, "plane", [(s, s + 1) for s in far])
-    corner = lax.ppermute(last, ("plane", "tile"), corners)
-    across = blur_across(raw_planes, blur_matrix())
-    grouped, single = column_tables()
+    last = last_planar(tile, last, edge, single)
+    last = lax.ppermute(last, "plane", [(s, s + 1) for s in near])
     meta = pair_table(pair_sections, pair_rows, pair_extent, owners)
-    last = last_planar(tile, across, halo, grouped)
-    last = lax.ppermute(last, "plane", [(s, s + 1) for s in near])
     spectra, head = row_spectra(tile, across, halo, grouped, row_transform_table())
     spectra = head_spectra(
         tile, slab, last, behind, corner, blur_matrix(), single, head,

time: 67.5 us -> 67 us (level); the launches traced: 66.5 us -> 66.8 us
  starting transfers between devices: 6.26 us -> 8.92 us
  waiting for transfers between devices: 4 us -> 2.24 us
  local copies, waits for them, and re-layouts: 1 us -> 0.07 us
    ppermute x1, waiting for transfers between devices: 2.73 us -> 0.01 us  [correlate(): halo = lax.ppermute(edges, 'tile', turns)]
    ppermute x1, starting transfers between devices: 0.69 us -> 2.92 us  [correlate(): halo = lax.ppermute(edges, 'tile', turns)]
    ppermute x2 -> x3, waiting for transfers between devices: 1.27 us -> 2.23 us  [the longest x1 2.23 us: correlate(): corner = lax.ppermute(raw_last, ('plane', 'tile'), corners)]
    squeeze x1 -> x0, local copies, waits for them, and re-layouts: 0.91 us -> none  [correlate(): last = raw_planes[raw_planes.shape[0] - 1]]
    ppermute x2 -> x3, starting transfers between devices: 2.7 us -> 3.27 us  [the longest x1 1.29 us: correlate(): behind = lax.ppermute(raw_last, 'plane', [(s, s + 1) for s in far])]
  transfers between devices with their start and end apart: 4 -> 5, of which waited for: 2 -> 1; matrix products, arithmetic and copies ran while one was open for 0% -> 0% of each run, Pallas kernels for 6% -> 5%
where the time goes in v3:
time: 67 us; the launch traced here: 66.8 us
  blocking collectives  46.1 us (69%)
  Pallas kernels  9.05 us (14%)
  starting transfers between devices  8.92 us (13%)
  waiting for transfers between devices  2.24 us (3%)
    all_to_all x1, blocking collectives, correlate(): lax.all_to_all(cross.reshape(TILES, OWN_CAP * 16, 128), 'tile', 0, 0, til...  25.5 us
    all_to_all x1, blocking collectives, correlate(): lax.all_to_all(spectra.reshape(TILES, 16, spectra.shape[1]), 'tile', 0, 0...  20.6 us
    ppermute x1, starting transfers between devices, correlate(): halo = lax.ppermute(edges, 'tile', turns)  2.92 us
    ppermute x1, starting transfers between devices, correlate(): last = lax.ppermute(last, 'plane', [(s, s + 1) for s in near])  2.73 us
    pallas_call x1, Pallas kernels, blur_across(): pl.pallas_call(across_kernel, in_specs=[whole()] * 2, out_specs=[whole()]...  2.32 us
    ppermute x1, waiting for transfers between devices, correlate(): corner = lax.ppermute(raw_last, ('plane', 'tile'), corners)  2.23 us
    pallas_call x1, Pallas kernels, surfaces(): pl.pallas_call(surface_kernel, in_specs=[whole()] * 4, out_specs=whole(pl...  2 us
    pallas_call x1, Pallas kernels, cross_spectra(): pl.pallas_call(cross_kernel, in_specs=[whole(pltpu.SMEM)] * 2 + [whole()]...  1.99 us
  transfers between devices with their start and end apart: 5, of which 1 were waited for; matrix products, arithmetic and copies ran while one was open for 0% of the time, Pallas kernels for 5%

profile of v3, /device:TPU:7, one launch (start us, length us, event | category | flops | bytes accessed | tf_op | source)
XLA Modules:
  0.0 66.8 jit_solution(7306535184418815395)
XLA Ops:
  0.0 0.0 copy-start.2
  0.0 0.0 copy-start.3
  0.0 0.0 copy-start.10
  0.0 0.0 copy-start.12
  0.1 1.3 %blur_last.1 = (bf16[32,512]{1,0:T(8,128)(2,1)S(1)}, bf16[32,256]{1,0:T(8,128)(2,1)S(1)}, bf16[8,256]{1,0:T(8,128)(2,1)S(1)}) custom-call(bf16[96,32,512]{2,1,0:T(8,128)(2,1)} %raw_ref.3, bf16[512,256]{1,0:T(8,128)(2,1)} %constant.32.clone.table_hbm.table_ref.blur_ref), custom_call_target="tpu_custom_call" | custom-call | tf_op jit(solution)/shard_map/blur_last/pallas_call | solution.py:143
  1.4 1.3 %collective-permute-start.2 = (bf16[32,512]{1,0:T(8,128)(2,1)S(1)}, bf16[32,512]{1,0:T(8,128)(2,1)S(1)}, u32[]{:S(2)}, u32[]{:S(2)}) collective-permute-start(bf16[32,512]{1,0:T(8,128)(2,1)S(1)} %get-tuple-element.16), channel_id=1, source_target_pairs={{112,128},{240,256},{368,384},{113,129},{241,257},{369,385},{114,1... | collective-permute-start | bytes 98312 | tf_op jit(solution)/shard_map/ppermute | solution.py:521
  2.7 1.3 %collective-permute-start.3 = (bf16[32,512]{1,0:T(8,128)(2,1)S(1)}, bf16[32,512]{1,0:T(8,128)(2,1)S(1)}, u32[]{:S(2)}, u32[]{:S(2)}) collective-permute-start(bf16[32,512]{1,0:T(8,128)(2,1)S(1)} %get-tuple-element.16), channel_id=1, source_target_pairs={{113,128},{114,129},{115,130},{116,131},{117,132},{118,133},{119,1... | collective-permute-start | bytes 98312 | tf_op jit(solution)/shard_map/ppermute | solution.py:520
  4.0 0.0 copy-start.6
  4.0 0.7 %collective-permute-start = (bf16[8,256]{1,0:T(8,128)(2,1)S(1)}, bf16[8,256]{1,0:T(8,128)(2,1)S(1)}, u32[]{:S(2)}, u32[]{:S(2)}) collective-permute-start(bf16[8,256]{1,0:T(8,128)(2,1)S(1)} %get-tuple-element.15), channel_id=1, source_target_pairs={{1,0},{2,1},{3,2},{4,3},{5,4},{6,5},{7,6},{8,7},{9,8},{10,9},{11,1... | collective-permute-start | bytes 12296 | tf_op jit(solution)/shard_map/ppermute | solution.py:522
  4.7 2.3 %blur_across.1 = (bf16[12,256,256]{2,1,0:T(8,128)(2,1)S(1)}, bf16[12,24,256]{2,1,0:T(8,128)(2,1)S(1)}) custom-call(bf16[96,32,512]{2,1,0:T(8,128)(2,1)S(1)} %copy-done, bf16[512,256]{1,0:T(8,128)(2,1)S(1)} %copy-done.1), custom_call_target="tpu_custom_call" | custom-call | flops 805306368 | bytes 4718592 | tf_op jit(solution)/shard_map/blur_across/pallas_call | solution.py:186
  7.0 2.9 %collective-permute-start.4 = (bf16[12,24,256]{2,1,0:T(8,128)(2,1)S(1)}, bf16[12,24,256]{2,1,0:T(8,128)(2,1)S(1)}, u32[]{:S(2)}, u32[]{:S(2)}) collective-permute-start(bf16[12,24,256]{2,1,0:T(8,128)(2,1)S(1)} %get-tuple-element.18), channel_id=1, source_target_pairs={{1,0},{2,1},{3,2},{4,3},{5,4},{6,5},{7,6},{8,7},{9,8},{10,9},{11,1... | collective-permute-start | bytes 442376 | tf_op jit(solution)/shard_map/ppermute | solution.py:524
  9.9 0.0 copy-done.12
  9.9 0.2 convert_reduce_fusion
  10.1 0.0 collective-permute-done.halo_ref
  10.2 0.0 copy-done.8
  10.2 0.1 last_planar.1
  10.3 2.7 %collective-permute-start.1 = (bf16[16,256]{1,0:T(8,128)(2,1)S(1)}, bf16[16,256]{1,0:T(8,128)(2,1)S(1)}, u32[]{:S(2)}, u32[]{:S(2)}) collective-permute-start(bf16[16,256]{1,0:T(8,128)(2,1)S(1)} %last_planar.1), channel_id=1, source_target_pairs={{0,16},{16,32},{32,48},{48,64},{64,80},{80,96},{96,112},{128,144},... | collective-permute-start | bytes 24584 | tf_op jit(solution)/shard_map/ppermute | solution.py:526
  13.0 0.0 collective-permute-done.4.halo_ref
  13.1 0.0 copy-start.4
  13.1 0.0 copy-start.5
  13.1 0.0 copy-start.7
  13.1 0.8 %row_spectra.1 = (bf16[256,768]{1,0:T(8,128)(2,1)S(1)}, bf16[17,16,256]{2,1,0:T(8,128)(2,1)S(1)}) custom-call(s32[1]{0:T(128)} %bitcast.tile_ref, bf16[12,256,256]{2,1,0:T(8,128)(2,1)S(1)} %get-tuple-element.17.across_ref, bf16[12,24,256]{2,1,0:T(8,128)(2,1)S(1)} %collective-permute-done.4.halo_ref, bf16[2,128,280]{2,1,0:T(8,128)(2,1)S(1)} %copy-done.3, ...), custom_call_target="tpu_custom_call" | custom-call | flops 226492416 | bytes 1572864 | tf_op jit(solution)/shard_map/row_spectra/pallas_call | solution.py:255
  13.9 0.0 collective-permute-done.1.next_ref
  13.9 0.0 collective-permute-done.2.behind_ref
  13.9 2.2 %collective-permute-done.3.corner_ref = bf16[32,512]{1,0:T(8,128)(2,1)S(1)} collective-permute-done((bf16[32,512]{1,0:T(8,128)(2,1)S(1)}, bf16[32,512]{1,0:T(8,128)(2,1)S(1)}, u32[]{:S(2)}, u32[]{:S(2)}) %collective-permute-start.3) | collective-permute-done | bytes 32800 | tf_op jit(solution)/shard_map/ppermute | solution.py:520
  16.1 0.6 head_spectra.1
  16.7 20.6 %all_to_all.10.spectra_ref = bf16[16,16,768]{2,1,0:T(8,128)(2,1)S(1)} all-to-all(bf16[16,16,768]{2,1,0:T(8,128)(2,1)S(1)} %bitcast.16), channel_id=1, replica_groups=mesh['plane'=32,'tile'=16] {'tile'}, dimensions={0} | all-to-all | bytes 786432 | tf_op jit(solution)/shard_map/all_to_all | solution.py:534
  37.3 0.0 copy-done.6
  37.3 2.0 %cross_spectra.1 = bf16[192,16,128]{2,1,0:T(8,128)(2,1)S(1)} custom-call(s32[1]{0:T(128)} %bitcast.tile_ref, s32[6,64]{1,0:T(8,128)S(1)} %pad_add_fusion.meta_ref, bf16[16,16,768]{2,1,0:T(8,128)(2,1)S(1)} %all_to_all.10.spectra_ref, bf16[128,256]{1,0:T(8,128)(2,1)S(1)} %copy-done.6), custom_call_target="tpu_custom_call" | custom-call | tf_op jit(solution)/shard_map/cross_spectra/pallas_call | solution.py:393
  39.3 25.5 %all_to_all.11 = bf16[16,192,128]{2,1,0:T(8,128)(2,1)S(1)} all-to-all(bf16[16,192,128]{2,1,0:T(8,128)(2,1)S(1)} %bitcast.15), channel_id=1, replica_groups=mesh['plane'=32,'tile'=16] {'tile'}, dimensions={0} | all-to-all | bytes 1572864 | tf_op jit(solution)/shard_map/all_to_all | solution.py:542
  64.8 0.0 copy-done.5
  64.8 2.0 %surfaces.1 = bf16[12,128,256]{2,1,0:T(8,128)(2,1)} custom-call(bf16[16,12,16,128]{3,2,1,0:T(8,128)(2,1)S(1)} %bitcast.14, bf16[128,128]{1,0:T(8,128)(2,1)S(1)} %copy-done.7, bf16[256,128]{1,0:T(8,128)(2,1)S(1)} %copy-done.5, bf16[256,256]{1,0:T(8,128)(2,1)S(1)} %copy-done.4), custom_call_target="tpu_custom_call" | custom-call | tf_op jit(solution)/shard_map/surfaces/pallas_call | solution.py:488
  (17 shorter events, 0.0 us)
Async XLA Ops:
  0.0 4.7 %copy-start.1 = (bf16[512,256]{1,0:T(8,128)(2,1)S(1)}, bf16[512,256]{1,0:T(8,128)(2,1)}, u32[]{:S(2)}) copy-start(bf16[512,256]{1,0:T(8,128)(2,1)} %constant.32.clone.table_hbm.table_ref.blur_ref) | copy-start | bytes 786436
  0.0 10.2 %copy-start.8 = (bf16[2,16,40]{2,1,0:T(8,128)(2,1)S(1)}, bf16[2,16,40]{2,1,0:T(8,128)(2,1)}, u32[]{:S(2)}) copy-start(bf16[2,16,40]{2,1,0:T(8,128)(2,1)} %constant.33.clone.single_ref) | copy-start | bytes 7684
  0.0 4.7 %copy-start = (bf16[96,32,512]{2,1,0:T(8,128)(2,1)S(1)}, bf16[96,32,512]{2,1,0:T(8,128)(2,1)}, u32[]{:S(2)}) copy-start(bf16[96,32,512]{2,1,0:T(8,128)(2,1)} %raw_ref.3) | copy-start | bytes 9437188
  0.0 13.0 %copy-start.2 = (bf16[256,256]{1,0:T(8,128)(2,1)S(1)}, bf16[256,256]{1,0:T(8,128)(2,1)}, u32[]{:S(2)}) copy-start(bf16[256,256]{1,0:T(8,128)(2,1)} %constant.35.clone.table_ref) | copy-start | bytes 393220
  0.0 13.0 %copy-start.3 = (bf16[2,128,280]{2,1,0:T(8,128)(2,1)S(1)}, bf16[2,128,280]{2,1,0:T(8,128)(2,1)}, u32[]{:S(2)}) copy-start(bf16[2,128,280]{2,1,0:T(8,128)(2,1)} %constant.34.clone.grouped_ref) | copy-start | bytes 430084
  0.0 9.9 %copy-start.10 = (s32[64,2]{0,1:T(2,128)S(1)}, s32[64,2]{0,1:T(2,128)}, u32[]{:S(2)}) copy-start(s32[64,2]{0,1:T(2,128)} %param.18) | copy-start | bytes 1540
  0.0 9.9 %copy-start.12 = (s32[64,1]{0,1:T(1,128)S(1)}, s32[64,1]{0,1:T(1,128)}, u32[]{:S(2)}) copy-start(s32[64,1]{0,1:T(1,128)} %param.20) | copy-start | bytes 772
  0.1 10.1 %copy-start.9 = (s32[64,2]{0,1:T(2,128)S(1)}, s32[64,2]{0,1:T(2,128)}, u32[]{:S(2)}) copy-start(s32[64,2]{0,1:T(2,128)} %param.17) | copy-start | bytes 1540
  0.1 10.1 %copy-start.11 = (s32[64]{0:T(128)S(1)}, s32[64]{0:T(128)}, u32[]{:S(2)}) copy-start(s32[64]{0:T(128)} %param.19) | copy-start | bytes 772
  1.4 12.5 %collective-permute-start.2 = (bf16[32,512]{1,0:T(8,128)(2,1)S(1)}, bf16[32,512]{1,0:T(8,128)(2,1)S(1)}, u32[]{:S(2)}, u32[]{:S(2)}) collective-permute-start(bf16[32,512]{1,0:T(8,128)(2,1)S(1)} %get-tuple-element.16), channel_id=1, source_target_pairs={{112,128},{240,256},{368,384},{113,129},{241,257},{369,385},{114,1... | collective-permute-start | bytes 98312 | tf_op jit(solution)/shard_map/ppermute | solution.py:521
  2.7 13.5 %collective-permute-start.3 = (bf16[32,512]{1,0:T(8,128)(2,1)S(1)}, bf16[32,512]{1,0:T(8,128)(2,1)S(1)}, u32[]{:S(2)}, u32[]{:S(2)}) collective-permute-start(bf16[32,512]{1,0:T(8,128)(2,1)S(1)} %get-tuple-element.16), channel_id=1, source_target_pairs={{113,128},{114,129},{115,130},{116,131},{117,132},{118,133},{119,1... | collective-permute-start | bytes 98312 | tf_op jit(solution)/shard_map/ppermute | solution.py:520
  4.0 33.4 %copy-start.6 = (bf16[128,256]{1,0:T(8,128)(2,1)S(1)}, bf16[128,256]{1,0:T(8,128)(2,1)}, u32[]{:S(2)}) copy-start(bf16[128,256]{1,0:T(8,128)(2,1)} %constant.36.clone.table_ref) | copy-start | bytes 196612
  4.0 6.2 %collective-permute-start = (bf16[8,256]{1,0:T(8,128)(2,1)S(1)}, bf16[8,256]{1,0:T(8,128)(2,1)S(1)}, u32[]{:S(2)}, u32[]{:S(2)}) collective-permute-start(bf16[8,256]{1,0:T(8,128)(2,1)S(1)} %get-tuple-element.15), channel_id=1, source_target_pairs={{1,0},{2,1},{3,2},{4,3},{5,4},{6,5},{7,6},{8,7},{9,8},{10,9},{11,1... | collective-permute-start | bytes 12296 | tf_op jit(solution)/shard_map/ppermute | solution.py:522
  7.0 6.0 %collective-permute-start.4 = (bf16[12,24,256]{2,1,0:T(8,128)(2,1)S(1)}, bf16[12,24,256]{2,1,0:T(8,128)(2,1)S(1)}, u32[]{:S(2)}, u32[]{:S(2)}) collective-permute-start(bf16[12,24,256]{2,1,0:T(8,128)(2,1)S(1)} %get-tuple-element.18), channel_id=1, source_target_pairs={{1,0},{2,1},{3,2},{4,3},{5,4},{6,5},{7,6},{8,7},{9,8},{10,9},{11,1... | collective-permute-start | bytes 442376 | tf_op jit(solution)/shard_map/ppermute | solution.py:524
  10.3 3.6 %collective-permute-start.1 = (bf16[16,256]{1,0:T(8,128)(2,1)S(1)}, bf16[16,256]{1,0:T(8,128)(2,1)S(1)}, u32[]{:S(2)}, u32[]{:S(2)}) collective-permute-start(bf16[16,256]{1,0:T(8,128)(2,1)S(1)} %last_planar.1), channel_id=1, source_target_pairs={{0,16},{16,32},{32,48},{48,64},{64,80},{80,96},{96,112},{128,144},... | collective-permute-start | bytes 24584 | tf_op jit(solution)/shard_map/ppermute | solution.py:526
  13.1 51.8 %copy-start.4 = (bf16[256,256]{1,0:T(8,128)(2,1)S(1)}, bf16[256,256]{1,0:T(8,128)(2,1)}, u32[]{:S(2)}) copy-start(bf16[256,256]{1,0:T(8,128)(2,1)} %constant.39.clone.row_ref) | copy-start | bytes 393220
  13.1 51.7 %copy-start.5 = (bf16[256,128]{1,0:T(8,128)(2,1)S(1)}, bf16[256,128]{1,0:T(8,128)(2,1)}, u32[]{:S(2)}) copy-start(bf16[256,128]{1,0:T(8,128)(2,1)} %constant.38.clone.column_ref) | copy-start | bytes 196612
  13.1 51.7 %copy-start.7 = (bf16[128,128]{1,0:T(8,128)(2,1)S(1)}, bf16[128,128]{1,0:T(8,128)(2,1)}, u32[]{:S(2)}) copy-start(bf16[128,128]{1,0:T(8,128)(2,1)} %constant.37.clone.reversal_ref) | copy-start | bytes 98308
